TPU v7x, 512 devices: a whole 4x8x8 slice. The times are simulated.
512 devices in a mesh: seg: 4 (over y_hi, core), pan: 128 (over y_lo, z, x).
Axes of the slice: x: 4, y: 8 (y_hi: 2, y_lo: 4; y = y_hi * 4 + y_lo), z: 8, core: 2. Of those that a mesh axis runs over, the one named last changes fastest.
Arguments:
- sources: bfloat16 [2, 2, 64, 1048576], P(None, None, 'seg', 'pan'), may hold values from -0.75 to 0.75
- panel_geom: float32 [6, 1048576], P(None, 'pan'), may hold values from -1 to 1, as said below
- mic_pos: float32 [3, 1024], replicated, may hold values from -12 to 12, as said below
- mic_order: int32 [1024], replicated, may hold values from 0 to 1023, each once
Outputs:
- csm: float32 [2, 1024, 1024], P(None, 'pan', 'seg')
Inputs may be any that keep to these rules, and one draw needn't show every extreme that they name: `mic_order`: each of the 1024 microphones stands exactly once. `panel_geom`: panel centres lie on a cylinder of radius 1 around the first axis with first coordinate within -1 to 1; normals are the unit radial directions. `mic_pos`: microphones lie at distances 6 to 12 from the anchor (0, 0, 0).
All inputs are finite; a program needn't handle non-finite values.
Results may differ from a plain program's by a relative error of at most 0.0039.
Values may be sent and summed in bfloat16 or wider, within the bound.
No kernel may reach another device: no remote copies, remote signals or barrier semaphores. Data moves between devices by JAX's collectives and lax.ppermute only.
A program may use at most 64 MiB of HBM per device.

v0:
```python
import math

import jax
import jax.numpy as jnp
from jax import lax
from jax.sharding import PartitionSpec as P

mach_number = 0.3
beta_sq = 0.91
wave_number = 40.0


def kernel_block(mics, geometry):
    dx = mics[0][:, None] - geometry[0][None, :]
    dy = mics[1][:, None] - geometry[1][None, :]
    dz = mics[2][:, None] - geometry[2][None, :]
    rstar = jnp.sqrt(dx * dx + beta_sq * (dy * dy + dz * dz))
    radius = (rstar - mach_number * dx) / beta_sq
    phase = wave_number * radius
    amplitude = 1.0 / (4.0 * math.pi * rstar)
    green_re = amplitude * jnp.cos(phase)
    green_im = -amplitude * jnp.sin(phase)
    normal_part = (
        dx * geometry[3][None, :] + dy * geometry[4][None, :] + dz * geometry[5][None, :]
    ) / rstar
    scale_re = normal_part / (wave_number * rstar)
    dip_re = scale_re * green_re - normal_part * green_im
    dip_im = scale_re * green_im + normal_part * green_re
    return jnp.concatenate([green_re, green_im, dip_re, dip_im], axis=1).astype(jnp.bfloat16)


def block_weights(piece):
    swapped = jnp.transpose(piece, (0, 1, 3, 2))
    real_cols = jnp.concatenate(
        [swapped[0, 0], -swapped[1, 0], swapped[0, 1], -swapped[1, 1]], axis=0
    )
    imag_cols = jnp.concatenate(
        [swapped[1, 0], swapped[0, 0], swapped[1, 1], swapped[0, 1]], axis=0
    )
    return jnp.concatenate([real_cols, imag_cols], axis=1)


def split_sources(sources, blocks, block_size):
    shaped = sources.reshape(2, 2, sources.shape[2], blocks, block_size)
    return jnp.transpose(shaped, (3, 0, 1, 2, 4))


def panel_spectra(mics, geom_blocks, source_blocks):

    def step(running, pair):
        geometry, piece = pair
        weights = block_weights(piece)
        return (
            running
            + jnp.dot(kernel_block(mics, geometry), weights, preferred_element_type=jnp.float32),
            None,
        )

    init = jnp.zeros((mics.shape[1], 2 * source_blocks.shape[3]), jnp.float32)
    summed, unused = lax.scan(step, init, (geom_blocks, source_blocks))
    return summed


def summed_spectra(mic_rows, geom_blocks, source_blocks):
    local_terms = panel_spectra(mic_rows, geom_blocks, source_blocks)
    return lax.psum(local_terms, "pan")


def cross_terms(own_rows, columns):
    half = columns.shape[1] // 2
    rows_re = own_rows[:, :half]
    rows_im = own_rows[:, half:]
    cols_re = columns[:, :half]
    cols_im = columns[:, half:]
    highest = lax.Precision.HIGHEST
    csm_re = jnp.dot(rows_re, cols_re.T, precision=highest) + jnp.dot(
        rows_im, cols_im.T, precision=highest
    )
    csm_im = jnp.dot(rows_im, cols_re.T, precision=highest) - jnp.dot(
        rows_re, cols_im.T, precision=highest
    )
    return jnp.stack([csm_re, csm_im])


def shards(sources, panel_geom, mic_pos, mic_order):
    ordered = jnp.take(mic_pos, mic_order, axis=1)
    panels_here = panel_geom.shape[1]
    block_size = min(512, panels_here)
    blocks = panels_here // block_size
    geom_blocks = jnp.transpose(panel_geom.reshape(6, blocks, block_size), (1, 0, 2))
    mics_all = ordered.shape[1]
    seg_count = lax.axis_size("seg")
    row_count = mics_all // lax.axis_size("pan")
    row_start = lax.axis_index("pan") * row_count
    source_blocks = split_sources(sources, blocks, block_size)
    spectra = summed_spectra(ordered, geom_blocks, source_blocks)
    own_rows = lax.dynamic_slice_in_dim(spectra, row_start, row_count, 0)
    partial_csm = cross_terms(own_rows, spectra)
    summed = lax.psum_scatter(partial_csm, "seg", scatter_dimension=2, tiled=True)
    return summed / (own_rows.shape[1] // 2 * seg_count)


def solution(mesh):
    placed = (P(None, None, "seg", "pan"), P(None, "pan"), P(), P())
    return jax.shard_map(
        shards, mesh=mesh, in_specs=placed, out_specs=P(None, "pan", "seg"), check_vma=False
    )
```

profile of v0, /device:TPU:1, one launch (start us, length us, event | category | flops | bytes accessed | tf_op | source)
XLA Modules:
  0.0 1561.1 jit_solution(7481023906343510673)
XLA Ops:
  9.0 2.8 gather_fusion
  14.1 267.6 %while.13 = (s32[]{:T(128)}, f32[1024,32]{0,1:T(8,128)S(1)}, f32[3,1024]{1,0:T(4,128)S(1)}, f32[16,6,512]{2,1,0:T(8,128)}, bf16[16,2,2,16,512]{4,3,2,1,0:T(8,128...) while((s32[]{:T(128)}, f32[1024,32]{0,1:T(8,128)S(1)}, ...), condition=%wide.region_1.2_spmd.clone, body=%wide.region_0.1_spmd.clone.sunk | while | flops 170999808 | bytes 9150687 | solution.py:60
  15.1 12.3 subtract_convert_fusion.2
  31.8 12.3 subtract_convert_fusion.2
  44.9 2.6 fusion.66
  48.5 12.3 subtract_convert_fusion.2
  65.2 12.3 subtract_convert_fusion.2
  78.4 2.6 fusion.66
  82.0 12.3 subtract_convert_fusion.2
  98.7 12.3 subtract_convert_fusion.2
  111.8 2.6 fusion.66
  115.4 12.3 subtract_convert_fusion.2
  128.6 2.6 fusion.66
  132.1 12.3 subtract_convert_fusion.2
  148.9 12.3 subtract_convert_fusion.2
  165.6 12.3 subtract_convert_fusion.2
  182.3 12.3 subtract_convert_fusion.2
  199.0 12.3 subtract_convert_fusion.2
  215.7 12.3 subtract_convert_fusion.2
  232.5 12.3 subtract_convert_fusion.2
  249.2 12.3 subtract_convert_fusion.2
  265.9 12.3 subtract_convert_fusion.2
  282.4 1203.3 %all-reduce.2.cloned.1.call-done = f32[1024,32]{0,1:T(8,128)} async-done(((f32[1024,32]{0,1:T(8,128)}), f32[1024,32]{0,1:T(8,128)}) %all-reduce.2.cloned.1.call-update) | async-done | bytes 131088 | tf_op jit(solution)/shard_map/psum | solution.py:66
  1491.1 61.8 %reduce-scatter.2.cloned.1.call-done = f32[2,8,256]{2,1,0:T(8,128)} async-done(((f32[2,8,1024]{2,1,0:T(8,128)}), f32[2,8,256]{2,1,0:T(8,128)}) %reduce-scatter.2.cloned.1.call-update) | async-done | bytes 16400 | tf_op jit(solution)/shard_map/reduce_scatter | solution.py:99
  (114 shorter events, 72.2 us)
Async XLA Ops:
  6.5 1479.1 %all-reduce.2.cloned.1.call-start = ((), (), s32[]{:S(2)}) async-start(), calls=%async_computation.1 | async-start | bytes 262144 | tf_op jit(solution)/shard_map/psum | solution.py:66
  7.9 4.2 copy-start
  281.7 0.7 copy-start.1
  282.3 1270.6 %reduce-scatter.2.cloned.1.call-start = ((), (), s32[]{:S(2)}) async-start(), calls=%async_computation.2 | async-start | bytes 81920 | tf_op jit(solution)/shard_map/reduce_scatter | solution.py:99
Sparse Core Ops, SparseCore 0:
  282.5 1203.1 all-reduce.1
  1491.2 61.6 reduce-scatter.1
where the time goes:
time: 1560 us
  waiting for transfers between devices  1270 us (81%)
  other arithmetic  200 us (13%)
  matrix products  45.8 us (3%)
  local copies, waits for them, and re-layouts  35.8 us (2%)
    psum x1, waiting for transfers between devices, summed_spectra(): return lax.psum(local_terms, 'pan')  1200 us
    another operation x16, other arithmetic  196 us
    reduce_scatter x1, waiting for transfers between devices, shards(): lax.psum_scatter(partial_csm, 'seg', scatter_dimension=2, tiled=True)  61.8 us
    dot_general x16, matrix products, step(): jnp.dot(kernel_block(mics, geometry), weights, preferred_element_type=jnp...  41.1 us
  transfers between devices with their start and end apart: 2, of which 2 were waited for; matrix products, arithmetic and copies ran while one was open for 0% of the time, Pallas kernels for 0%

commit v1 on v0

v1 whole, which is shorter than its diff:
```python
import functools
import math

import jax
import jax.numpy as jnp
from jax import lax
from jax.experimental import pallas as pl
from jax.experimental.pallas import tpu as pltpu
from jax.sharding import Mesh, PartitionSpec as P

mach_number = 0.3
beta_sq = 0.91
wave_number = 40.0
turns = wave_number / (beta_sq * 2.0 * math.pi)
half_sine = (4.44284725189209, -7.306909084320068, 3.5908987522125244, -0.7760252356529236)

f32 = jnp.float32
bf16 = jnp.bfloat16
PAN = ("yl", "z", "x")
tile = 256


def split3(value):
    high = value.astype(bf16).astype(f32)
    rest = value - high
    middle = rest.astype(bf16).astype(f32)
    return high, middle, (rest - middle).astype(bf16).astype(f32)


def zero_rows(count, width):
    return jnp.zeros((count, width), f32)


def mic_features(order_ref, mic_ref, feature_ref):
    mics = mic_ref[...]
    total = mics.shape[1]
    parts = jnp.concatenate([*split3(mics), zero_rows(7, total)], 0).astype(bf16)
    for start in range(0, total, tile):
        wanted = order_ref[:, start : start + tile]
        ids = lax.broadcasted_iota(jnp.int32, (total, tile), 0)
        chosen = jnp.where(ids == wanted, 1.0, 0.0).astype(bf16)
        picked = jnp.dot(parts, chosen, preferred_element_type=f32)
        high, middle, low = picked[0:3], picked[3:6], picked[6:9]
        full = high + middle + low
        square = (turns * turns) * (
            full[0:1] * full[0:1] + beta_sq * (full[1:2] * full[1:2] + full[2:3] * full[2:3])
        )
        shift = (-mach_number * turns) * full[0:1]
        ones = jnp.ones((3, tile), f32)
        rows = [high, high, middle, high, middle, low, ones, *split3(square), *split3(shift)]
        rows.append(zero_rows(37, tile))
        feature_ref[start : start + tile, :] = jnp.concatenate(rows, 0).T.astype(bf16)


def panel_features(geometry):
    centre, normal = geometry[0:3], geometry[3:6]
    width = geometry.shape[1]
    scale = turns * turns
    cross = jnp.concatenate(
        [centre[0:1] * (-2.0 * scale), centre[1:3] * (-2.0 * beta_sq * scale)], 0
    )
    square = scale * (
        centre[0:1] * centre[0:1]
        + beta_sq * (centre[1:2] * centre[1:2] + centre[2:3] * centre[2:3])
    )
    product = centre * normal
    offset = (-turns) * (product[0:1] + product[1:2] + product[2:3])
    shift = (mach_number * turns) * centre[0:1]
    ch, cm, cl = split3(cross)
    nh, nm, nl = split3(turns * normal)
    ones = jnp.ones((3, width), f32)

    def stack(*rows):
        used = sum(row.shape[0] for row in rows)
        return jnp.concatenate([*rows, zero_rows(64 - used, width)], 0).astype(bf16)

    distance = stack(ch, cm, ch, cl, cm, ch, *split3(square), ones)
    along = stack(nh, nm, nh, nl, nm, nh, *split3(offset))
    moved = stack(zero_rows(18, width), *split3(shift), zero_rows(3, width), ones)
    return distance, along, moved


def kernel_values(distance, along, moved):
    inverse = lax.rsqrt(distance)
    phase = distance * inverse + moved
    part = phase - jnp.round(phase)
    square = part * part
    a0, a1, a2, a3 = half_sine
    sine = part * (a0 + square * (a1 + square * (a2 + square * a3)))
    cos_all = 1.0 - sine * sine
    rest = cos_all + 1.0
    sin_all = sine * (rest * lax.rsqrt(rest))
    amplitude = inverse * (turns / (4.0 * math.pi))
    green_re = amplitude * cos_all
    green_im = amplitude * sin_all
    near = inverse * (turns / wave_number)
    normal_part = along * inverse
    dip_re = normal_part * (near * green_re + green_im)
    dip_im = normal_part * (green_re - near * green_im)
    return green_re, green_im, dip_re, dip_im


def spectra_kernel(core_ref, own_ref, other_ref, geom_ref, mic_ref, order_ref, out_ref,
                   feature_ref, total_ref, kernel_ref, weight_ref):
    panels = other_ref.shape[3]
    mics = mic_ref.shape[1]
    core = core_ref[0]
    mic_features(order_ref, mic_ref, feature_ref)
    total_ref[...] = jnp.zeros_like(total_ref)

    def step(index, carry):
        here = pl.multiple_of(core * panels + index * tile, tile)
        there = pl.multiple_of(index * tile, tile)
        distance_rows, along_rows, moved_rows = panel_features(geom_ref[:, pl.ds(here, tile)])

        def both(part, kind):
            own = own_ref[part, kind, :, pl.ds(here, tile)]
            other = other_ref[part, kind, :, pl.ds(there, tile)]
            return [jnp.where(core == 0, own, other), jnp.where(core == 0, other, own)]

        mono_re, mono_im, dip_re, dip_im = both(0, 0), both(1, 0), both(0, 1), both(1, 1)
        blocks = (
            mono_re + mono_im,
            mono_im + [-x for x in mono_re],
            dip_re + dip_im,
            [-x for x in dip_im] + dip_re,
        )
        for place, block in enumerate(blocks):
            weight_ref[:, place * tile : (place + 1) * tile] = jnp.concatenate(block, 0)
        features = feature_ref[...]
        values = kernel_values(
            jnp.dot(features, distance_rows, preferred_element_type=f32),
            jnp.dot(features, along_rows, preferred_element_type=f32),
            jnp.dot(features, moved_rows, preferred_element_type=f32),
        )
        for place, value in enumerate(values):
            kernel_ref[:, place * tile : (place + 1) * tile] = value.astype(bf16)
        total_ref[...] += lax.dot_general(
            kernel_ref[...], weight_ref[...], (((1,), (1,)), ((), ())), preferred_element_type=f32
        )
        return carry

    lax.fori_loop(0, panels // tile, step, 0)
    rows = mics // 8
    for pair in range(4):
        first = total_ref[(2 * pair) * rows : (2 * pair + 1) * rows]
        second = total_ref[(2 * pair + 1) * rows : (2 * pair + 2) * rows]
        block = jnp.concatenate([first, second], 1)
        out_ref[:rows, pair, :] = block
        out_ref[rows:, pair, :] = block


def partial_spectra(core, own, other, geometry, mic_pos, order):
    mics = mic_pos.shape[1]
    vmem = pl.BlockSpec(memory_space=pltpu.VMEM)
    return pl.pallas_call(
        spectra_kernel,
        out_shape=jax.ShapeDtypeStruct((mics // 4, 4, 128), f32),
        in_specs=[pl.BlockSpec(memory_space=pltpu.SMEM)] + [vmem] * 5,
        out_specs=vmem,
        scratch_shapes=[
            pltpu.VMEM((mics, 64), bf16),
            pltpu.VMEM((mics, 64), f32),
            pltpu.VMEM((mics, 4 * tile), bf16),
            pltpu.VMEM((64, 4 * tile), bf16),
        ],
        compiler_params=pltpu.CompilerParams(vmem_limit_bytes=40 << 20),
    )(core, own, other, geometry, mic_pos, order)


def shards(sources, panel_geom, mic_pos, mic_order):
    core = lax.axis_index("core")
    half = sources.shape[3] // 2
    away = lax.dynamic_slice_in_dim(sources, (1 - core) * half, half, 3)
    other = lax.ppermute(away, "core", [(0, 1), (1, 0)])
    order = mic_order.reshape(-1, 8).T.reshape(1, -1)
    partial = partial_spectra(
        core.astype(jnp.int32).reshape(1), sources, other, panel_geom, mic_pos, order
    )
    arrived = lax.all_to_all(partial, ("core", *PAN), 0, 0, tiled=True)
    owned = jnp.sum(arrived, axis=0)
    spread = jnp.broadcast_to(owned[None], arrived.shape)
    gathered = lax.all_to_all(spread, ("yh", *PAN), 0, 0, tiled=True)
    pan = lax.axis_index(PAN)
    quarter = lax.axis_index("yh") * 2 + core
    peers = gathered.shape[0] // 2
    gathered = gathered.reshape(2, peers, 4, 128)
    rows = lax.dynamic_slice_in_dim(gathered, pan, 1, 1).reshape(2, 8, 64)
    columns = lax.dynamic_slice_in_dim(gathered, quarter * (peers // 4), peers // 4, 1)
    columns = columns.reshape(2, 2 * peers, 64)
    turned = jnp.concatenate([rows[..., 32:], -rows[..., :32]], 2)
    left = jnp.concatenate([rows, turned], 1)
    csm = lax.dot_general(
        left, columns, (((0, 2), (0, 2)), ((), ())), precision=lax.Precision.HIGHEST
    )
    return csm.reshape(2, 8, -1) / 64


def solution(mesh):
    fine = Mesh(mesh.devices.reshape(2, 2, 4, 8, 4), ("yh", "core", *PAN))
    seg = ("yh", "core")
    placed = (P(None, None, seg, PAN), P(None, PAN), P(), P())
    return jax.shard_map(
        shards, mesh=fine, in_specs=placed, out_specs=P(None, PAN, seg), check_vma=False
    )
```

time: 1560 us -> 107 us (0.07)
  waiting for transfers between devices: 1270 us -> 18.5 us
  other arithmetic: 200 us -> 0.35 us
  matrix products: 45.8 us -> 0.94 us
  blocking collectives: 0 us -> 34.2 us
  local copies, waits for them, and re-layouts: 35.8 us -> 3.36 us
  Pallas kernels: 0 us -> 28.9 us
  starting transfers between devices: 0.04 us -> 18.4 us
    psum x1 -> x0, waiting for transfers between devices: 1200 us -> none  [summed_spectra(): return lax.psum(local_terms, 'pan')]
    another operation x17 -> x0, other arithmetic: 197 us -> none
    reduce_scatter x1 -> x0, waiting for transfers between devices: 61.8 us -> none  [shards(): lax.psum_scatter(partial_csm, 'seg', scatter_dimension=2, tiled=True)]
    dot_general x20 -> x1, matrix products: 45.8 us -> 0.94 us  [shards(): lax.dot_general(left, columns, (((0, 2), (0, 2)), ((), ())), precision=la...]
    all_to_all x0 -> x1, blocking collectives: none -> 34.2 us  [shards(): arrived = lax.all_to_all(partial, ('core', *PAN), 0, 0, tiled=True)]
    pallas_call x0 -> x1, Pallas kernels: none -> 28.9 us  [partial_spectra(): pl.pallas_call(spectra_kernel, out_shape=jax.ShapeDtypeStruct((mics // 4,...]
    all_to_all x0 -> x1, waiting for transfers between devices: none -> 17.1 us  [shards(): gathered = lax.all_to_all(spread, ('yh', *PAN), 0, 0, tiled=True)]
where the time goes in v1:
time: 107 us; the launch traced here: 105 us
  blocking collectives  34.2 us (32%)
  Pallas kernels  28.9 us (27%)
  waiting for transfers between devices  18.5 us (17%)
  starting transfers between devices  18.4 us (17%)
  local copies, waits for them, and re-layouts  3.36 us (3%)
    all_to_all x1, blocking collectives, shards(): arrived = lax.all_to_all(partial, ('core', *PAN), 0, 0, tiled=True)  34.2 us
    pallas_call x1, Pallas kernels, partial_spectra(): pl.pallas_call(spectra_kernel, out_shape=jax.ShapeDtypeStruct((mics // 4,...  28.9 us
    all_to_all x1, waiting for transfers between devices, shards(): gathered = lax.all_to_all(spread, ('yh', *PAN), 0, 0, tiled=True)  17.1 us
    all_to_all x1, starting transfers between devices, shards(): gathered = lax.all_to_all(spread, ('yh', *PAN), 0, 0, tiled=True)  9.62 us
    ppermute x1, starting transfers between devices, shards(): other = lax.ppermute(away, 'core', [(0, 1), (1, 0)])  8.79 us
  transfers between devices with their start and end apart: 2, of which 2 were waited for; matrix products, arithmetic and copies ran while one was open for 0% of the time, Pallas kernels for 0%

profile of v1, /device:TPU:1, one launch (start us, length us, event | category | flops | bytes accessed | tf_op | source)
XLA Modules:
  0.0 104.8 jit_solution(9386173877245321063)
XLA Ops:
  0.0 0.0 copy-start
  0.0 0.0 copy-start.3
  0.0 1.2 %constant_dynamic-slice_fusion.2 = bf16[2,2,16,4096]{3,2,1,0:T(8,128)(2,1)S(1)} fusion(bf16[2,2,16,8192]{3,2,1,0:T(8,128)(2,1)} %own_ref.1, s32[]{:T(128)S(6)} %select_n.9), kind=kLoop, calls=%fused_computation.11 | loop fusion | bytes 1048580 | tf_op jit(solution)/shard_map/dynamic_slice | solution.py:174
  1.2 8.8 %collective-permute-start = (bf16[2,2,16,4096]{3,2,1,0:T(8,128)(2,1)S(1)}, bf16[2,2,16,4096]{3,2,1,0:T(8,128)(2,1)S(1)}, u32[]{:S(2)}, u32[]{:S(2)}) collective-permute-start(bf16[2,2,16,4096]{3,2,1,0:T(8,128)(2,1)S(1)} %constant_dynamic-slice_fusion.2), channel_id=1, source_target_pairs={{0,128},{128,0},{1,129},{129,1},{2,130},{130,2},{3,131},{131,3},{4... | collective-permute-start | bytes 1572872 | tf_op jit(solution)/shard_map/ppermute | solution.py:175
  10.0 0.0 copy-done.3
  10.0 0.1 reshape.22
  10.1 0.0 copy-start.2
  10.1 1.4 %collective-permute-done.other_ref = bf16[2,2,16,4096]{3,2,1,0:T(8,128)(2,1)S(1)} collective-permute-done((bf16[2,2,16,4096]{3,2,1,0:T(8,128)(2,1)S(1)}, bf16[2,2,16,4096]{3,2,1,0:T(8,128)(2,1)S(1)}, u32[]{:S(2)}, u32[]{:S(2)}) %collective-permute-start) | collective-permute-done | bytes 524320 | tf_op jit(solution)/shard_map/ppermute | solution.py:175
  11.5 0.0 copy-done
  11.5 0.0 copy-done.2
  11.5 0.0 copy-start.1
  11.5 0.9 copy-done.1
  12.5 28.9 %shard_map.46 = f32[256,4,128]{2,1,0:T(4,128)S(1)} custom-call(s32[1]{0:T(128)} %bitcast.core_ref, bf16[2,2,16,8192]{3,2,1,0:T(8,128)(2,1)S(1)} %copy-done, bf16[2,2,16,4096]{3,2,1,0:T(8,128)(2,1)S(1)} %collective-permute-done.other_ref, f32[6,8192]{1,0:T(8,128)S(1)} %copy-done.1, f32[3,1024]{1,0:T(4,128)S(1)} %copy-done.2, s32[1,1024]{1,0:T(1,128)S(1)} %bitcast.18), custom_call_target="tpu_custom_call" | custom-call | tf_op jit(solution)/shard_map/pallas_call | solution.py:156
  41.4 34.2 %all_to_all.10 = f32[256,4,128]{2,1,0:T(4,128)S(1)} all-to-all(f32[256,4,128]{2,1,0:T(4,128)S(1)} %shard_map.46), channel_id=1, replica_groups=mesh['yh'=2,'core'=2,'yl'=4,'z'=8,'x'=4] {'core','yl','z','x'}, dimensions={0} | all-to-all | bytes 1048576 | tf_op jit(solution)/shard_map/all_to_all | solution.py:180
  75.6 0.3 reduce_sum.9
  75.9 0.9 broadcast_in_dim.2
  76.7 9.6 %all-to-all-start.1 = ((f32[256,4,128]{2,1,0:T(4,128)}), f32[256,4,128]{2,1,0:T(4,128)S(1)}, u32[]{:S(2)}, u32[]{:S(2)}) async-start(f32[256,4,128]{2,1,0:T(4,128)} %broadcast_in_dim.2), calls=%async_computation.1 | async-start | bytes 1048576 | tf_op jit(solution)/shard_map/all_to_all | solution.py:183
  86.4 17.1 %all-to-all-done.1 = f32[256,4,128]{2,1,0:T(4,128)S(1)} async-done(((f32[256,4,128]{2,1,0:T(4,128)}), f32[256,4,128]{2,1,0:T(4,128)S(1)}, u32[]{:S(2)}, u32[]{:S(2)}) %all-to-all-start.1) | async-done | bytes 524320 | tf_op jit(solution)/shard_map/all_to_all | solution.py:183
  103.5 0.1 reshape.26
  103.7 0.1 reshape.25
  103.8 0.1 fusion.7
  103.8 0.9 fusion
  (3 shorter events, 0.1 us)
Async XLA Ops:
  0.0 11.5 %copy-start = (bf16[2,2,16,8192]{3,2,1,0:T(8,128)(2,1)S(1)}, bf16[2,2,16,8192]{3,2,1,0:T(8,128)(2,1)}, u32[]{:S(2)}) copy-start(bf16[2,2,16,8192]{3,2,1,0:T(8,128)(2,1)} %own_ref.1) | copy-start | bytes 3145732
  0.0 10.0 %copy-start.3 = (s32[1024]{0:T(1024)S(1)}, s32[1024]{0:T(1024)}, u32[]{:S(2)}) copy-start(s32[1024]{0:T(1024)} %param.7) | copy-start | bytes 12292
  1.2 10.3 %collective-permute-start = (bf16[2,2,16,4096]{3,2,1,0:T(8,128)(2,1)S(1)}, bf16[2,2,16,4096]{3,2,1,0:T(8,128)(2,1)S(1)}, u32[]{:S(2)}, u32[]{:S(2)}) collective-permute-start(bf16[2,2,16,4096]{3,2,1,0:T(8,128)(2,1)S(1)} %constant_dynamic-slice_fusion.2), channel_id=1, source_target_pairs={{0,128},{128,0},{1,129},{129,1},{2,130},{130,2},{3,131},{131,3},{4... | collective-permute-start | bytes 1572872 | tf_op jit(solution)/shard_map/ppermute | solution.py:175
  10.1 1.4 %copy-start.2 = (f32[3,1024]{1,0:T(4,128)S(1)}, f32[3,1024]{1,0:T(4,128)}, u32[]{:S(2)}) copy-start(f32[3,1024]{1,0:T(4,128)} %mic_ref.1) | copy-start | bytes 36868
  11.5 1.0 copy-start.1
  76.7 26.8 %all-to-all-start.1 = ((f32[256,4,128]{2,1,0:T(4,128)}), f32[256,4,128]{2,1,0:T(4,128)S(1)}, u32[]{:S(2)}, u32[]{:S(2)}) async-start(f32[256,4,128]{2,1,0:T(4,128)} %broadcast_in_dim.2), calls=%async_computation.1 | async-start | bytes 1048576 | tf_op jit(solution)/shard_map/all_to_all | solution.py:183

commit v2 on v1

--- a/solution.py
+++ b/solution.py
@@ -141,13 +141,9 @@
         return carry
 
     lax.fori_loop(0, panels // tile, step, 0)
-    rows = mics // 8
-    for pair in range(4):
-        first = total_ref[(2 * pair) * rows : (2 * pair + 1) * rows]
-        second = total_ref[(2 * pair + 1) * rows : (2 * pair + 2) * rows]
-        block = jnp.concatenate([first, second], 1)
-        out_ref[:rows, pair, :] = block
-        out_ref[rows:, pair, :] = block
+    half = mics // 2
+    both_halves = jnp.concatenate([total_ref[:half], total_ref[half:]], 1)
+    out_ref[...] = both_halves.reshape(out_ref.shape)
 
 
 def partial_spectra(core, own, other, geometry, mic_pos, order):
@@ -155,7 +151,7 @@
     vmem = pl.BlockSpec(memory_space=pltpu.VMEM)
     return pl.pallas_call(
         spectra_kernel,
-        out_shape=jax.ShapeDtypeStruct((mics // 4, 4, 128), f32),
+        out_shape=jax.ShapeDtypeStruct((32, mics // 64, 128), f32),
         in_specs=[pl.BlockSpec(memory_space=pltpu.SMEM)] + [vmem] * 5,
         out_specs=vmem,
         scratch_shapes=[
@@ -173,25 +169,25 @@
     half = sources.shape[3] // 2
     away = lax.dynamic_slice_in_dim(sources, (1 - core) * half, half, 3)
     other = lax.ppermute(away, "core", [(0, 1), (1, 0)])
-    order = mic_order.reshape(-1, 8).T.reshape(1, -1)
+    order = mic_order.reshape(2, 2, 32, 8).transpose(0, 2, 1, 3).reshape(1, -1)
     partial = partial_spectra(
         core.astype(jnp.int32).reshape(1), sources, other, panel_geom, mic_pos, order
     )
-    arrived = lax.all_to_all(partial, ("core", *PAN), 0, 0, tiled=True)
-    owned = jnp.sum(arrived, axis=0)
-    spread = jnp.broadcast_to(owned[None], arrived.shape)
-    gathered = lax.all_to_all(spread, ("yh", *PAN), 0, 0, tiled=True)
-    pan = lax.axis_index(PAN)
-    quarter = lax.axis_index("yh") * 2 + core
-    peers = gathered.shape[0] // 2
-    gathered = gathered.reshape(2, peers, 4, 128)
-    rows = lax.dynamic_slice_in_dim(gathered, pan, 1, 1).reshape(2, 8, 64)
-    columns = lax.dynamic_slice_in_dim(gathered, quarter * (peers // 4), peers // 4, 1)
-    columns = columns.reshape(2, 2 * peers, 64)
+    kept = jnp.sum(lax.all_to_all(partial, ("z", "x"), 0, 0, tiled=True), axis=0)
+    quarters = kept.reshape(2, 8, 2, 64).transpose(2, 0, 1, 3).reshape(4, 8, 64)
+    for_columns = jnp.repeat(quarters, 4, axis=0)
+    for_rows = jnp.tile(quarters, (4, 1, 1))
+    terms = jnp.concatenate([for_columns, for_rows], 2)
+    terms = lax.all_to_all(terms, ("yh", "core", "yl"), 0, 0, tiled=True)
+    joined = jnp.sum(terms.reshape(2, 8, 8, 128), axis=1)
+    rows = joined[:, :, 64:]
+    own_columns = joined[:, :, :64].transpose(1, 0, 2).reshape(8, 128)
+    spread = jnp.broadcast_to(own_columns[None], (32, 8, 128))
+    columns = lax.all_to_all(spread, ("z", "x"), 0, 0, tiled=True).reshape(256, 128)
     turned = jnp.concatenate([rows[..., 32:], -rows[..., :32]], 2)
-    left = jnp.concatenate([rows, turned], 1)
+    left = jnp.concatenate([rows, turned], 1).transpose(1, 0, 2).reshape(16, 128)
     csm = lax.dot_general(
-        left, columns, (((0, 2), (0, 2)), ((), ())), precision=lax.Precision.HIGHEST
+        left, columns, (((1,), (1,)), ((), ())), precision=lax.Precision.HIGHEST
     )
     return csm.reshape(2, 8, -1) / 64
 

time: 107 us -> 92 us (0.86); the launches traced: 105 us -> 91.7 us
  waiting for transfers between devices: 18.5 us -> 10.8 us
  starting transfers between devices: 18.4 us -> 12.8 us
  blocking collectives: 34.2 us -> 35.7 us
    all_to_all x1, waiting for transfers between devices: 17.1 us -> 9.58 us  [shards(): lax.all_to_all(spread, ('z', 'x'), 0, 0, tiled=True).reshape(256, 128)]
    all_to_all x1, starting transfers between devices: 9.62 us -> 3.84 us  [shards(): lax.all_to_all(spread, ('z', 'x'), 0, 0, tiled=True).reshape(256, 128)]
    all_to_all x1 -> x2, blocking collectives: 34.2 us -> 35.7 us  [the longest x1 18.9 us: shards(): lax.all_to_all(partial, ('z', 'x'), 0, 0, tiled=True)]
  transfers between devices with their start and end apart: 2 -> 2, of which waited for: 2 -> 2; matrix products, arithmetic and copies ran while one was open for 0% -> 1% of each run, Pallas kernels for 0% -> 0%
where the time goes in v2:
time: 92 us; the launch traced here: 91.7 us
  blocking collectives  35.7 us (39%)
  Pallas kernels  28.8 us (31%)
  starting transfers between devices  12.8 us (14%)
  waiting for transfers between devices  10.8 us (12%)
  local copies, waits for them, and re-layouts  2.47 us (3%)
    pallas_call x1, Pallas kernels, partial_spectra(): pl.pallas_call(spectra_kernel, out_shape=jax.ShapeDtypeStruct((32, mics /...  28.8 us
    all_to_all x1, blocking collectives, shards(): lax.all_to_all(partial, ('z', 'x'), 0, 0, tiled=True)  18.9 us
    all_to_all x1, blocking collectives, shards(): terms = lax.all_to_all(terms, ('yh', 'core', 'yl'), 0, 0, tiled=True)  16.8 us
    all_to_all x1, waiting for transfers between devices, shards(): lax.all_to_all(spread, ('z', 'x'), 0, 0, tiled=True).reshape(256, 128)  9.58 us
    ppermute x1, starting transfers between devices, shards(): other = lax.ppermute(away, 'core', [(0, 1), (1, 0)])  8.92 us
    all_to_all x1, starting transfers between devices, shards(): lax.all_to_all(spread, ('z', 'x'), 0, 0, tiled=True).reshape(256, 128)  3.84 us
  transfers between devices with their start and end apart: 2, of which 2 were waited for; matrix products, arithmetic and copies ran while one was open for 1% of the time, Pallas kernels for 0%

profile of v2, /device:TPU:1, one launch (start us, length us, event | category | flops | bytes accessed | tf_op | source)
XLA Modules:
  0.0 91.7 jit_solution(11238007266323555635)
XLA Ops:
  0.0 1.2 %constant_dynamic-slice_fusion = bf16[2,2,16,4096]{3,2,1,0:T(8,128)(2,1)S(1)} fusion(bf16[2,2,16,8192]{3,2,1,0:T(8,128)(2,1)} %own_ref.1, s32[]{:T(128)S(6)} %select_n.3), kind=kLoop, calls=%fused_computation.7 | loop fusion | bytes 1048580 | tf_op jit(solution)/shard_map/dynamic_slice | solution.py:170
  1.2 0.0 copy-start.1
  1.2 8.9 %collective-permute-start = (bf16[2,2,16,4096]{3,2,1,0:T(8,128)(2,1)S(1)}, bf16[2,2,16,4096]{3,2,1,0:T(8,128)(2,1)S(1)}, u32[]{:S(2)}, u32[]{:S(2)}) collective-permute-start(bf16[2,2,16,4096]{3,2,1,0:T(8,128)(2,1)S(1)} %constant_dynamic-slice_fusion), channel_id=1, source_target_pairs={{0,128},{128,0},{1,129},{129,1},{2,130},{130,2},{3,131},{131,3},{4... | collective-permute-start | bytes 1572872 | tf_op jit(solution)/shard_map/ppermute | solution.py:171
  10.1 0.0 copy-done.3
  10.1 0.1 reshape.34
  10.2 0.1 copy.11
  10.3 0.1 reshape.35.order_ref
  10.4 1.2 %collective-permute-done.other_ref = bf16[2,2,16,4096]{3,2,1,0:T(8,128)(2,1)S(1)} collective-permute-done((bf16[2,2,16,4096]{3,2,1,0:T(8,128)(2,1)S(1)}, bf16[2,2,16,4096]{3,2,1,0:T(8,128)(2,1)S(1)}, u32[]{:S(2)}, u32[]{:S(2)}) %collective-permute-start) | collective-permute-done | bytes 524320 | tf_op jit(solution)/shard_map/ppermute | solution.py:171
  11.6 0.0 copy-done
  11.6 0.0 copy-done.2
  11.6 28.8 %shard_map.46 = f32[32,16,128]{2,1,0:T(8,128)S(1)} custom-call(s32[1]{0:T(128)} %bitcast.core_ref, bf16[2,2,16,8192]{3,2,1,0:T(8,128)(2,1)S(1)} %copy-done, bf16[2,2,16,4096]{3,2,1,0:T(8,128)(2,1)S(1)} %collective-permute-done.other_ref, f32[6,8192]{1,0:T(8,128)S(1)} %copy-done.1, f32[3,1024]{1,0:T(4,128)S(1)} %copy-done.2, s32[1,1024]{1,0:T(1,128)S(1)} %reshape.35.order_ref), custom_call_target="tpu_custom_call" | custom-call | tf_op jit(solution)/shard_map/pallas_call | solution.py:152
  40.4 18.9 %all_to_all.15 = f32[32,16,128]{2,1,0:T(8,128)S(1)} all-to-all(f32[32,16,128]{2,1,0:T(8,128)S(1)} %shard_map.46), channel_id=1, replica_groups=mesh['yh'=2,'core'=2,'yl'=4,'z'=8,'x'=4] {'z','x'}, dimensions={0} | all-to-all | bytes 524288 | tf_op jit(solution)/shard_map/all_to_all | solution.py:176
  59.3 0.1 reshape.36
  59.4 0.1 pad_maximum_fusion
  59.5 16.8 %all_to_all.16 = f32[16,8,128]{2,1,0:T(8,128)S(1)} all-to-all(f32[16,8,128]{2,1,0:T(8,128)S(1)} %pad_maximum_fusion), channel_id=1, replica_groups=mesh['yh'=2,'core'=2,'yl'=4,'z'=8,'x'=4] {'yh','core','yl'}, dimensions={0} | all-to-all | bytes 131072 | tf_op jit(solution)/shard_map/all_to_all | solution.py:181
  76.4 0.1 slice_bitcast_fusion
  76.4 0.1 broadcast_in_dim.11
  76.5 0.7 broadcast_in_dim.12
  77.2 3.8 %all-to-all-start.2 = ((f32[32,8,128]{2,1,0:T(8,128)}), f32[32,8,128]{2,1,0:T(8,128)S(1)}, u32[]{:S(2)}, u32[]{:S(2)}) async-start(f32[32,8,128]{2,1,0:T(8,128)} %broadcast_in_dim.12), calls=%async_computation.2 | async-start | bytes 262144 | tf_op jit(solution)/shard_map/all_to_all | solution.py:186
  81.0 0.1 fusion.1
  81.1 0.1 maximum_bitcast_fusion
  81.2 0.1 dot_general.5
  81.3 9.6 %all-to-all-done.2 = f32[32,8,128]{2,1,0:T(8,128)S(1)} async-done(((f32[32,8,128]{2,1,0:T(8,128)}), f32[32,8,128]{2,1,0:T(8,128)S(1)}, u32[]{:S(2)}, u32[]{:S(2)}) %all-to-all-start.2) | async-done | bytes 131104 | tf_op jit(solution)/shard_map/all_to_all | solution.py:186
  90.9 0.8 convolution_multiply_fusion
  (11 shorter events, 0.1 us)
Async XLA Ops:
  0.0 11.6 %copy-start = (bf16[2,2,16,8192]{3,2,1,0:T(8,128)(2,1)S(1)}, bf16[2,2,16,8192]{3,2,1,0:T(8,128)(2,1)}, u32[]{:S(2)}) copy-start(bf16[2,2,16,8192]{3,2,1,0:T(8,128)(2,1)} %own_ref.1) | copy-start | bytes 3145732
  0.0 10.1 %copy-start.3 = (s32[1024]{0:T(1024)S(1)}, s32[1024]{0:T(1024)}, u32[]{:S(2)}) copy-start(s32[1024]{0:T(1024)} %param.7) | copy-start | bytes 12292
  0.0 11.6 %copy-start.2 = (f32[3,1024]{1,0:T(4,128)S(1)}, f32[3,1024]{1,0:T(4,128)}, u32[]{:S(2)}) copy-start(f32[3,1024]{1,0:T(4,128)} %mic_ref.1) | copy-start | bytes 36868
  1.2 10.5 %copy-start.1 = (f32[6,8192]{1,0:T(8,128)S(1)}, f32[6,8192]{1,0:T(8,128)}, u32[]{:S(2)}) copy-start(f32[6,8192]{1,0:T(8,128)} %geom_ref.1) | copy-start | bytes 589828
  1.2 10.4 %collective-permute-start = (bf16[2,2,16,4096]{3,2,1,0:T(8,128)(2,1)S(1)}, bf16[2,2,16,4096]{3,2,1,0:T(8,128)(2,1)S(1)}, u32[]{:S(2)}, u32[]{:S(2)}) collective-permute-start(bf16[2,2,16,4096]{3,2,1,0:T(8,128)(2,1)S(1)} %constant_dynamic-slice_fusion), channel_id=1, source_target_pairs={{0,128},{128,0},{1,129},{129,1},{2,130},{130,2},{3,131},{131,3},{4... | collective-permute-start | bytes 1572872 | tf_op jit(solution)/shard_map/ppermute | solution.py:171
  77.2 13.7 %all-to-all-start.2 = ((f32[32,8,128]{2,1,0:T(8,128)}), f32[32,8,128]{2,1,0:T(8,128)S(1)}, u32[]{:S(2)}, u32[]{:S(2)}) async-start(f32[32,8,128]{2,1,0:T(8,128)} %broadcast_in_dim.12), calls=%async_computation.2 | async-start | bytes 262144 | tf_op jit(solution)/shard_map/all_to_all | solution.py:186

commit v3 on v2

--- a/solution.py
+++ b/solution.py
@@ -13,11 +13,15 @@
 wave_number = 40.0
 turns = wave_number / (beta_sq * 2.0 * math.pi)
 half_sine = (4.44284725189209, -7.306909084320068, 3.5908987522125244, -0.7760252356529236)
+strength = turns / (4.0 * math.pi)
+scaled_sine = tuple(math.sqrt(strength) * value for value in half_sine)
 
 f32 = jnp.float32
 bf16 = jnp.bfloat16
 PAN = ("yl", "z", "x")
 tile = 256
+chunk = 512
+unroll = 4
 
 
 def split3(value):
@@ -85,14 +89,13 @@
     phase = distance * inverse + moved
     part = phase - jnp.round(phase)
     square = part * part
-    a0, a1, a2, a3 = half_sine
+    a0, a1, a2, a3 = scaled_sine
     sine = part * (a0 + square * (a1 + square * (a2 + square * a3)))
-    cos_all = 1.0 - sine * sine
-    rest = cos_all + 1.0
+    cos_all = strength - sine * sine
+    rest = cos_all + strength
     sin_all = sine * (rest * lax.rsqrt(rest))
-    amplitude = inverse * (turns / (4.0 * math.pi))
-    green_re = amplitude * cos_all
-    green_im = amplitude * sin_all
+    green_re = inverse * cos_all
+    green_im = inverse * sin_all
     near = inverse * (turns / wave_number)
     normal_part = along * inverse
     dip_re = normal_part * (near * green_re + green_im)
@@ -101,14 +104,14 @@
 
 
 def spectra_kernel(core_ref, own_ref, other_ref, geom_ref, mic_ref, order_ref, out_ref,
-                   feature_ref, total_ref, kernel_ref, weight_ref):
+                   feature_ref, total_ref, *buffers):
     panels = other_ref.shape[3]
     mics = mic_ref.shape[1]
     core = core_ref[0]
     mic_features(order_ref, mic_ref, feature_ref)
     total_ref[...] = jnp.zeros_like(total_ref)
 
-    def step(index, carry):
+    def block_of_panels(index, kernel_ref, weight_ref):
         here = pl.multiple_of(core * panels + index * tile, tile)
         there = pl.multiple_of(index * tile, tile)
         distance_rows, along_rows, moved_rows = panel_features(geom_ref[:, pl.ds(here, tile)])
@@ -127,20 +130,25 @@
         )
         for place, block in enumerate(blocks):
             weight_ref[:, place * tile : (place + 1) * tile] = jnp.concatenate(block, 0)
-        features = feature_ref[...]
-        values = kernel_values(
-            jnp.dot(features, distance_rows, preferred_element_type=f32),
-            jnp.dot(features, along_rows, preferred_element_type=f32),
-            jnp.dot(features, moved_rows, preferred_element_type=f32),
-        )
-        for place, value in enumerate(values):
-            kernel_ref[:, place * tile : (place + 1) * tile] = value.astype(bf16)
+        for start in range(0, mics, chunk):
+            rows = slice(start, start + chunk)
+            features = feature_ref[rows]
+            distance = jnp.dot(features, distance_rows, preferred_element_type=f32)
+            moved = jnp.dot(features, moved_rows, preferred_element_type=f32)
+            along = jnp.dot(features, along_rows, preferred_element_type=f32)
+            for place, value in enumerate(kernel_values(distance, along, moved)):
+                kernel_ref[rows, place * tile : (place + 1) * tile] = value.astype(bf16)
         total_ref[...] += lax.dot_general(
             kernel_ref[...], weight_ref[...], (((1,), (1,)), ((), ())), preferred_element_type=f32
         )
+
+    def step(index, carry):
+        for part in range(unroll):
+            kernel_ref, weight_ref = buffers[2 * (part % 2) : 2 * (part % 2) + 2]
+            block_of_panels(unroll * index + part, kernel_ref, weight_ref)
         return carry
 
-    lax.fori_loop(0, panels // tile, step, 0)
+    lax.fori_loop(0, panels // (unroll * tile), step, 0)
     half = mics // 2
     both_halves = jnp.concatenate([total_ref[:half], total_ref[half:]], 1)
     out_ref[...] = both_halves.reshape(out_ref.shape)
@@ -157,9 +165,8 @@
         scratch_shapes=[
             pltpu.VMEM((mics, 64), bf16),
             pltpu.VMEM((mics, 64), f32),
-            pltpu.VMEM((mics, 4 * tile), bf16),
-            pltpu.VMEM((64, 4 * tile), bf16),
-        ],
+        ]
+        + [pltpu.VMEM((mics, 4 * tile), bf16), pltpu.VMEM((64, 4 * tile), bf16)] * 2,
         compiler_params=pltpu.CompilerParams(vmem_limit_bytes=40 << 20),
     )(core, own, other, geometry, mic_pos, order)
 

time: 92 us -> 89.3 us (0.971)
  Pallas kernels: 28.8 us -> 26.1 us
    pallas_call x1, Pallas kernels: 28.8 us -> 26.1 us  [partial_spectra(): pl.pallas_call(spectra_kernel, out_shape=jax.ShapeDtypeStruct((32, mics /...]
where the time goes in v3:
time: 89.3 us; the launch traced here: 89 us
  blocking collectives  35.7 us (40%)
  Pallas kernels  26.1 us (29%)
  starting transfers between devices  12.8 us (14%)
  waiting for transfers between devices  10.8 us (12%)
  local copies, waits for them, and re-layouts  2.47 us (3%)
    pallas_call x1, Pallas kernels, partial_spectra(): pl.pallas_call(spectra_kernel, out_shape=jax.ShapeDtypeStruct((32, mics /...  26.1 us
    all_to_all x1, blocking collectives, shards(): lax.all_to_all(partial, ('z', 'x'), 0, 0, tiled=True)  18.9 us
    all_to_all x1, blocking collectives, shards(): terms = lax.all_to_all(terms, ('yh', 'core', 'yl'), 0, 0, tiled=True)  16.8 us
    all_to_all x1, waiting for transfers between devices, shards(): lax.all_to_all(spread, ('z', 'x'), 0, 0, tiled=True).reshape(256, 128)  9.55 us
    ppermute x1, starting transfers between devices, shards(): other = lax.ppermute(away, 'core', [(0, 1), (1, 0)])  8.92 us
    all_to_all x1, starting transfers between devices, shards(): lax.all_to_all(spread, ('z', 'x'), 0, 0, tiled=True).reshape(256, 128)  3.84 us
  transfers between devices with their start and end apart: 2, of which 2 were waited for; matrix products, arithmetic and copies ran while one was open for 1% of the time, Pallas kernels for 0%

profile of v3, /device:TPU:1, one launch (start us, length us, event | category | flops | bytes accessed | tf_op | source)
XLA Modules:
  0.0 89.0 jit_solution(11303386308195743431)
XLA Ops:
  0.0 1.2 %constant_dynamic-slice_fusion = bf16[2,2,16,4096]{3,2,1,0:T(8,128)(2,1)S(1)} fusion(bf16[2,2,16,8192]{3,2,1,0:T(8,128)(2,1)} %own_ref.1, s32[]{:T(128)S(6)} %select_n.3), kind=kLoop, calls=%fused_computation.7 | loop fusion | bytes 1048580 | tf_op jit(solution)/shard_map/dynamic_slice | solution.py:177
  1.2 0.0 copy-start.1
  1.2 8.9 %collective-permute-start = (bf16[2,2,16,4096]{3,2,1,0:T(8,128)(2,1)S(1)}, bf16[2,2,16,4096]{3,2,1,0:T(8,128)(2,1)S(1)}, u32[]{:S(2)}, u32[]{:S(2)}) collective-permute-start(bf16[2,2,16,4096]{3,2,1,0:T(8,128)(2,1)S(1)} %constant_dynamic-slice_fusion), channel_id=1, source_target_pairs={{0,128},{128,0},{1,129},{129,1},{2,130},{130,2},{3,131},{131,3},{4... | collective-permute-start | bytes 1572872 | tf_op jit(solution)/shard_map/ppermute | solution.py:178
  10.1 0.0 copy-done.3
  10.1 0.1 reshape.34
  10.2 0.1 copy.11
  10.3 0.1 reshape.35.order_ref
  10.4 1.2 %collective-permute-done.other_ref = bf16[2,2,16,4096]{3,2,1,0:T(8,128)(2,1)S(1)} collective-permute-done((bf16[2,2,16,4096]{3,2,1,0:T(8,128)(2,1)S(1)}, bf16[2,2,16,4096]{3,2,1,0:T(8,128)(2,1)S(1)}, u32[]{:S(2)}, u32[]{:S(2)}) %collective-permute-start) | collective-permute-done | bytes 524320 | tf_op jit(solution)/shard_map/ppermute | solution.py:178
  11.6 0.0 copy-done
  11.6 0.0 copy-done.2
  11.6 26.1 %shard_map.46 = f32[32,16,128]{2,1,0:T(8,128)S(1)} custom-call(s32[1]{0:T(128)} %bitcast.core_ref, bf16[2,2,16,8192]{3,2,1,0:T(8,128)(2,1)S(1)} %copy-done, bf16[2,2,16,4096]{3,2,1,0:T(8,128)(2,1)S(1)} %collective-permute-done.other_ref, f32[6,8192]{1,0:T(8,128)S(1)} %copy-done.1, f32[3,1024]{1,0:T(4,128)S(1)} %copy-done.2, s32[1,1024]{1,0:T(1,128)S(1)} %reshape.35.order_ref), custom_call_target="tpu_custom_call" | custom-call | tf_op jit(solution)/shard_map/pallas_call | solution.py:160
  37.7 18.9 %all_to_all.15 = f32[32,16,128]{2,1,0:T(8,128)S(1)} all-to-all(f32[32,16,128]{2,1,0:T(8,128)S(1)} %shard_map.46), channel_id=1, replica_groups=mesh['yh'=2,'core'=2,'yl'=4,'z'=8,'x'=4] {'z','x'}, dimensions={0} | all-to-all | bytes 524288 | tf_op jit(solution)/shard_map/all_to_all | solution.py:183
  56.6 0.1 reshape.36
  56.7 0.1 pad_maximum_fusion
  56.8 16.8 %all_to_all.16 = f32[16,8,128]{2,1,0:T(8,128)S(1)} all-to-all(f32[16,8,128]{2,1,0:T(8,128)S(1)} %pad_maximum_fusion), channel_id=1, replica_groups=mesh['yh'=2,'core'=2,'yl'=4,'z'=8,'x'=4] {'yh','core','yl'}, dimensions={0} | all-to-all | bytes 131072 | tf_op jit(solution)/shard_map/all_to_all | solution.py:188
  73.7 0.1 slice_bitcast_fusion
  73.7 0.1 broadcast_in_dim.11
  73.8 0.7 broadcast_in_dim.12
  74.5 3.8 %all-to-all-start.2 = ((f32[32,8,128]{2,1,0:T(8,128)}), f32[32,8,128]{2,1,0:T(8,128)S(1)}, u32[]{:S(2)}, u32[]{:S(2)}) async-start(f32[32,8,128]{2,1,0:T(8,128)} %broadcast_in_dim.12), calls=%async_computation.2 | async-start | bytes 262144 | tf_op jit(solution)/shard_map/all_to_all | solution.py:193
  78.3 0.1 fusion.1
  78.4 0.1 maximum_bitcast_fusion
  78.5 0.1 dot_general.5
  78.6 9.6 %all-to-all-done.2 = f32[32,8,128]{2,1,0:T(8,128)S(1)} async-done(((f32[32,8,128]{2,1,0:T(8,128)}), f32[32,8,128]{2,1,0:T(8,128)S(1)}, u32[]{:S(2)}, u32[]{:S(2)}) %all-to-all-start.2) | async-done | bytes 131104 | tf_op jit(solution)/shard_map/all_to_all | solution.py:193
  88.1 0.8 convolution_multiply_fusion
  (11 shorter events, 0.1 us)
Async XLA Ops:
  0.0 11.6 %copy-start = (bf16[2,2,16,8192]{3,2,1,0:T(8,128)(2,1)S(1)}, bf16[2,2,16,8192]{3,2,1,0:T(8,128)(2,1)}, u32[]{:S(2)}) copy-start(bf16[2,2,16,8192]{3,2,1,0:T(8,128)(2,1)} %own_ref.1) | copy-start | bytes 3145732
  0.0 10.1 %copy-start.3 = (s32[1024]{0:T(1024)S(1)}, s32[1024]{0:T(1024)}, u32[]{:S(2)}) copy-start(s32[1024]{0:T(1024)} %param.7) | copy-start | bytes 12292
  0.0 11.6 %copy-start.2 = (f32[3,1024]{1,0:T(4,128)S(1)}, f32[3,1024]{1,0:T(4,128)}, u32[]{:S(2)}) copy-start(f32[3,1024]{1,0:T(4,128)} %mic_ref.1) | copy-start | bytes 36868
  1.2 10.5 %copy-start.1 = (f32[6,8192]{1,0:T(8,128)S(1)}, f32[6,8192]{1,0:T(8,128)}, u32[]{:S(2)}) copy-start(f32[6,8192]{1,0:T(8,128)} %geom_ref.1) | copy-start | bytes 589828
  1.2 10.4 %collective-permute-start = (bf16[2,2,16,4096]{3,2,1,0:T(8,128)(2,1)S(1)}, bf16[2,2,16,4096]{3,2,1,0:T(8,128)(2,1)S(1)}, u32[]{:S(2)}, u32[]{:S(2)}) collective-permute-start(bf16[2,2,16,4096]{3,2,1,0:T(8,128)(2,1)S(1)} %constant_dynamic-slice_fusion), channel_id=1, source_target_pairs={{0,128},{128,0},{1,129},{129,1},{2,130},{130,2},{3,131},{131,3},{4... | collective-permute-start | bytes 1572872 | tf_op jit(solution)/shard_map/ppermute | solution.py:178
  74.5 13.7 %all-to-all-start.2 = ((f32[32,8,128]{2,1,0:T(8,128)}), f32[32,8,128]{2,1,0:T(8,128)S(1)}, u32[]{:S(2)}, u32[]{:S(2)}) async-start(f32[32,8,128]{2,1,0:T(8,128)} %broadcast_in_dim.12), calls=%async_computation.2 | async-start | bytes 262144 | tf_op jit(solution)/shard_map/all_to_all | solution.py:193

commit v4 on v3

--- a/solution.py
+++ b/solution.py
@@ -103,22 +103,32 @@
     return green_re, green_im, dip_re, dip_im
 
 
-def spectra_kernel(core_ref, own_ref, other_ref, geom_ref, mic_ref, order_ref, out_ref,
-                   feature_ref, total_ref, *buffers):
-    panels = other_ref.shape[3]
-    mics = mic_ref.shape[1]
+def prepare_kernel(core_ref, geom_ref, mic_ref, order_ref, feature_ref, *panel_refs):
+    mic_features(order_ref, mic_ref, feature_ref)
+    panels = panel_refs[0].shape[1]
+    for start in range(0, panels, chunk):
+        here = pl.multiple_of(core_ref[0] * panels + start, chunk)
+        for ref, rows in zip(panel_refs, panel_features(geom_ref[:, pl.ds(here, chunk)])):
+            ref[:, start : start + chunk] = rows
+
+
+def spectra_kernel(core_ref, own_ref, other_ref, feature_ref, distance_ref, along_ref, moved_ref,
+                   out_ref, total_ref, *buffers):
+    panels = distance_ref.shape[1]
+    mics = feature_ref.shape[0]
     core = core_ref[0]
-    mic_features(order_ref, mic_ref, feature_ref)
     total_ref[...] = jnp.zeros_like(total_ref)
 
     def block_of_panels(index, kernel_ref, weight_ref):
         here = pl.multiple_of(core * panels + index * tile, tile)
-        there = pl.multiple_of(index * tile, tile)
-        distance_rows, along_rows, moved_rows = panel_features(geom_ref[:, pl.ds(here, tile)])
+        columns = pl.ds(pl.multiple_of(index * tile, tile), tile)
+        distance_rows, along_rows, moved_rows = (
+            ref[:, columns] for ref in (distance_ref, along_ref, moved_ref)
+        )
 
         def both(part, kind):
             own = own_ref[part, kind, :, pl.ds(here, tile)]
-            other = other_ref[part, kind, :, pl.ds(there, tile)]
+            other = other_ref[part, kind, :, pl.ds(here, tile)]
             return [jnp.where(core == 0, own, other), jnp.where(core == 0, other, own)]
 
         mono_re, mono_im, dip_re, dip_im = both(0, 0), both(1, 0), both(0, 1), both(1, 1)
@@ -154,32 +164,46 @@
     out_ref[...] = both_halves.reshape(out_ref.shape)
 
 
-def partial_spectra(core, own, other, geometry, mic_pos, order):
+vmem = pl.BlockSpec(memory_space=pltpu.VMEM)
+smem = pl.BlockSpec(memory_space=pltpu.SMEM)
+
+
+def prepared(core, geometry, mic_pos, order):
     mics = mic_pos.shape[1]
-    vmem = pl.BlockSpec(memory_space=pltpu.VMEM)
+    panels = geometry.shape[1] // 2
+    rows = jax.ShapeDtypeStruct((64, panels), bf16)
+    return pl.pallas_call(
+        prepare_kernel,
+        out_shape=[jax.ShapeDtypeStruct((mics, 64), bf16), rows, rows, rows],
+        in_specs=[smem] + [vmem] * 3,
+        out_specs=[vmem] * 4,
+        compiler_params=pltpu.CompilerParams(vmem_limit_bytes=16 << 20),
+        cost_estimate=pl.CostEstimate(
+            flops=2 * 10**9, bytes_accessed=3000000, transcendentals=0
+        ),
+    )(core, geometry, mic_pos, order)
+
+
+def partial_spectra(core, own, other, features):
+    mics = features[0].shape[0]
     return pl.pallas_call(
         spectra_kernel,
         out_shape=jax.ShapeDtypeStruct((32, mics // 64, 128), f32),
-        in_specs=[pl.BlockSpec(memory_space=pltpu.SMEM)] + [vmem] * 5,
+        in_specs=[smem] + [vmem] * 6,
         out_specs=vmem,
-        scratch_shapes=[
-            pltpu.VMEM((mics, 64), bf16),
-            pltpu.VMEM((mics, 64), f32),
-        ]
+        scratch_shapes=[pltpu.VMEM((mics, 64), f32)]
         + [pltpu.VMEM((mics, 4 * tile), bf16), pltpu.VMEM((64, 4 * tile), bf16)] * 2,
-        compiler_params=pltpu.CompilerParams(vmem_limit_bytes=40 << 20),
-    )(core, own, other, geometry, mic_pos, order)
+        compiler_params=pltpu.CompilerParams(vmem_limit_bytes=32 << 20),
+    )(core, own, other, *features)
 
 
 def shards(sources, panel_geom, mic_pos, mic_order):
     core = lax.axis_index("core")
-    half = sources.shape[3] // 2
-    away = lax.dynamic_slice_in_dim(sources, (1 - core) * half, half, 3)
-    other = lax.ppermute(away, "core", [(0, 1), (1, 0)])
+    other = lax.ppermute(sources, "core", [(0, 1), (1, 0)])
     order = mic_order.reshape(2, 2, 32, 8).transpose(0, 2, 1, 3).reshape(1, -1)
-    partial = partial_spectra(
-        core.astype(jnp.int32).reshape(1), sources, other, panel_geom, mic_pos, order
-    )
+    which = core.astype(jnp.int32).reshape(1)
+    features = prepared(which, panel_geom, mic_pos, order)
+    partial = partial_spectra(which, sources, other, features)
     kept = jnp.sum(lax.all_to_all(partial, ("z", "x"), 0, 0, tiled=True), axis=0)
     quarters = kept.reshape(2, 8, 2, 64).transpose(2, 0, 1, 3).reshape(4, 8, 64)
     for_columns = jnp.repeat(quarters, 4, axis=0)

time: 89.3 us -> 90.8 us (1.017)
  Pallas kernels: 26.1 us -> 28.5 us
  waiting for transfers between devices: 10.8 us -> 9.55 us
    pallas_call x1, Pallas kernels: 26.1 us -> 27.4 us  [partial_spectra(): pl.pallas_call(spectra_kernel, out_shape=jax.ShapeDtypeStruct((32, mics /...]
    ppermute x1, waiting for transfers between devices: 1.22 us -> 0.01 us  [shards(): other = lax.ppermute(sources, 'core', [(0, 1), (1, 0)])]
    dynamic_slice x1 -> x0, local copies, waits for them, and re-layouts: 1.17 us -> none  [shards(): away = lax.dynamic_slice_in_dim(sources, (1 - core) * half, half, 3)]
    pallas_call x0 -> x1, Pallas kernels: none -> 1.1 us  [prepared(): pl.pallas_call(prepare_kernel, out_shape=[jax.ShapeDtypeStruct((mics, 64)...]
  transfers between devices with their start and end apart: 2 -> 2, of which waited for: 2 -> 1; matrix products, arithmetic and copies ran while one was open for 1% -> 1% of each run, Pallas kernels for 0% -> 1%
where the time goes in v4:
time: 90.8 us; the launch traced here: 90.4 us
  blocking collectives  35.8 us (39%)
  Pallas kernels  28.5 us (31%)
  starting transfers between devices  12.8 us (14%)
  waiting for transfers between devices  9.55 us (11%)
  local copies, waits for them, and re-layouts  2.65 us (3%)
    pallas_call x1, Pallas kernels, partial_spectra(): pl.pallas_call(spectra_kernel, out_shape=jax.ShapeDtypeStruct((32, mics /...  27.4 us
    all_to_all x1, blocking collectives, shards(): lax.all_to_all(partial, ('z', 'x'), 0, 0, tiled=True)  19.3 us
    all_to_all x1, blocking collectives, shards(): terms = lax.all_to_all(terms, ('yh', 'core', 'yl'), 0, 0, tiled=True)  16.5 us
    all_to_all x1, waiting for transfers between devices, shards(): lax.all_to_all(spread, ('z', 'x'), 0, 0, tiled=True).reshape(256, 128)  9.55 us
    ppermute x1, starting transfers between devices, shards(): other = lax.ppermute(sources, 'core', [(0, 1), (1, 0)])  8.91 us
    all_to_all x1, starting transfers between devices, shards(): lax.all_to_all(spread, ('z', 'x'), 0, 0, tiled=True).reshape(256, 128)  3.84 us
  transfers between devices with their start and end apart: 2, of which 1 were waited for; matrix products, arithmetic and copies ran while one was open for 1% of the time, Pallas kernels for 1%

profile of v4, /device:TPU:1, one launch (start us, length us, event | category | flops | bytes accessed | tf_op | source)
XLA Modules:
  0.0 90.4 jit_solution(13889719332703630140)
XLA Ops:
  0.0 8.9 %collective-permute-start = (bf16[2,2,16,8192]{3,2,1,0:T(8,128)(2,1)}, bf16[2,2,16,8192]{3,2,1,0:T(8,128)(2,1)S(1)}, u32[]{:S(2)}, u32[]{:S(2)}) collective-permute-start(bf16[2,2,16,8192]{3,2,1,0:T(8,128)(2,1)} %own_ref.1), channel_id=1, source_target_pairs={{0,128},{128,0},{1,129},{129,1},{2,130},{130,2},{3,131},{131,3},{4... | collective-permute-start | bytes 3145736 | tf_op jit(solution)/shard_map/ppermute | solution.py:202
  8.9 0.8 reshape.34
  9.7 0.1 copy.11
  9.8 0.0 copy-start.2
  9.8 0.1 reshape.35.order_ref
  9.9 0.0 copy-done.1
  9.9 0.6 copy-done.2
  10.5 1.1 %shard_map.46 = (bf16[1024,64]{1,0:T(8,128)(2,1)S(1)}, bf16[64,4096]{1,0:T(8,128)(2,1)S(1)}, bf16[64,4096]{1,0:T(8,128)(2,1)S(1)}, bf16[64,4096]{1,0:T(8,128)(2,1)S(1)}) custom-call(s32[1]{0:T(128)} %bitcast.core_ref, f32[6,8192]{1,0:T(8,128)S(1)} %copy-done.1, f32[3,1024]{1,0:T(4,128)S(1)} %copy-done.2, s32[1,1024]{1,0:T(1,128)S(1)} %reshape.35.order_ref), custom_call_target="tpu_custom_call" | custom-call | flops 2000000000 | bytes 3000000 | tf_op jit(solution)/shard_map/pallas_call | solution.py:175
  11.6 0.0 collective-permute-done.other_ref
  11.6 0.1 copy-done
  11.7 27.4 %shard_map.47 = f32[32,16,128]{2,1,0:T(8,128)S(1)} custom-call(s32[1]{0:T(128)} %bitcast.core_ref, bf16[2,2,16,8192]{3,2,1,0:T(8,128)(2,1)S(1)} %copy-done, bf16[2,2,16,8192]{3,2,1,0:T(8,128)(2,1)S(1)} %collective-permute-done.other_ref, bf16[1024,64]{1,0:T(8,128)(2,1)S(1)} %get-tuple-element.9.feature_ref, ...), custom_call_target="tpu_custom_call" | custom-call | tf_op jit(solution)/shard_map/pallas_call | solution.py:189
  39.1 19.3 %all_to_all.15 = f32[32,16,128]{2,1,0:T(8,128)S(1)} all-to-all(f32[32,16,128]{2,1,0:T(8,128)S(1)} %shard_map.47), channel_id=1, replica_groups=mesh['yh'=2,'core'=2,'yl'=4,'z'=8,'x'=4] {'z','x'}, dimensions={0} | all-to-all | bytes 524288 | tf_op jit(solution)/shard_map/all_to_all | solution.py:207
  58.4 0.1 reshape.36
  58.5 0.1 pad_maximum_fusion
  58.6 16.5 %all_to_all.16 = f32[16,8,128]{2,1,0:T(8,128)S(1)} all-to-all(f32[16,8,128]{2,1,0:T(8,128)S(1)} %pad_maximum_fusion), channel_id=1, replica_groups=mesh['yh'=2,'core'=2,'yl'=4,'z'=8,'x'=4] {'yh','core','yl'}, dimensions={0} | all-to-all | bytes 131072 | tf_op jit(solution)/shard_map/all_to_all | solution.py:212
  75.1 0.1 slice_bitcast_fusion
  75.2 0.1 broadcast_in_dim.11
  75.3 0.7 broadcast_in_dim.12
  76.0 3.8 %all-to-all-start.2 = ((f32[32,8,128]{2,1,0:T(8,128)}), f32[32,8,128]{2,1,0:T(8,128)S(1)}, u32[]{:S(2)}, u32[]{:S(2)}) async-start(f32[32,8,128]{2,1,0:T(8,128)} %broadcast_in_dim.12), calls=%async_computation.2 | async-start | bytes 262144 | tf_op jit(solution)/shard_map/all_to_all | solution.py:217
  79.8 0.1 fusion.1
  79.9 0.1 maximum_bitcast_fusion
  80.0 0.1 dot_general.5
  80.1 9.5 %all-to-all-done.2 = f32[32,8,128]{2,1,0:T(8,128)S(1)} async-done(((f32[32,8,128]{2,1,0:T(8,128)}), f32[32,8,128]{2,1,0:T(8,128)S(1)}, u32[]{:S(2)}, u32[]{:S(2)}) %all-to-all-start.2) | async-done | bytes 131104 | tf_op jit(solution)/shard_map/all_to_all | solution.py:217
  89.6 0.8 convolution_multiply_fusion
  (9 shorter events, 0.1 us)
Async XLA Ops:
  0.0 9.9 %copy-start.1 = (f32[6,8192]{1,0:T(8,128)S(1)}, f32[6,8192]{1,0:T(8,128)}, u32[]{:S(2)}) copy-start(f32[6,8192]{1,0:T(8,128)} %geom_ref.1) | copy-start | bytes 589828
  0.0 11.6 %collective-permute-start = (bf16[2,2,16,8192]{3,2,1,0:T(8,128)(2,1)}, bf16[2,2,16,8192]{3,2,1,0:T(8,128)(2,1)S(1)}, u32[]{:S(2)}, u32[]{:S(2)}) collective-permute-start(bf16[2,2,16,8192]{3,2,1,0:T(8,128)(2,1)} %own_ref.1), channel_id=1, source_target_pairs={{0,128},{128,0},{1,129},{129,1},{2,130},{130,2},{3,131},{131,3},{4... | collective-permute-start | bytes 3145736 | tf_op jit(solution)/shard_map/ppermute | solution.py:202
  9.8 0.7 copy-start.2
  10.5 1.2 %copy-start = (bf16[2,2,16,8192]{3,2,1,0:T(8,128)(2,1)S(1)}, bf16[2,2,16,8192]{3,2,1,0:T(8,128)(2,1)}, u32[]{:S(2)}) copy-start(bf16[2,2,16,8192]{3,2,1,0:T(8,128)(2,1)} %own_ref.1) | copy-start | bytes 3145732
  76.0 13.6 %all-to-all-start.2 = ((f32[32,8,128]{2,1,0:T(8,128)}), f32[32,8,128]{2,1,0:T(8,128)S(1)}, u32[]{:S(2)}, u32[]{:S(2)}) async-start(f32[32,8,128]{2,1,0:T(8,128)} %broadcast_in_dim.12), calls=%async_computation.2 | async-start | bytes 262144 | tf_op jit(solution)/shard_map/all_to_all | solution.py:217

commit v5 on v4

--- a/solution.py
+++ b/solution.py
@@ -98,33 +98,23 @@
     green_im = inverse * sin_all
     near = inverse * (turns / wave_number)
     normal_part = along * inverse
-    dip_re = normal_part * (near * green_re + green_im)
-    dip_im = normal_part * (green_re - near * green_im)
+    part_re = normal_part * green_re
+    part_im = normal_part * green_im
+    dip_re = near * part_re + part_im
+    dip_im = part_re - near * part_im
     return green_re, green_im, dip_re, dip_im
 
 
-def prepare_kernel(core_ref, geom_ref, mic_ref, order_ref, feature_ref, *panel_refs):
-    mic_features(order_ref, mic_ref, feature_ref)
-    panels = panel_refs[0].shape[1]
-    for start in range(0, panels, chunk):
-        here = pl.multiple_of(core_ref[0] * panels + start, chunk)
-        for ref, rows in zip(panel_refs, panel_features(geom_ref[:, pl.ds(here, chunk)])):
-            ref[:, start : start + chunk] = rows
-
-
-def spectra_kernel(core_ref, own_ref, other_ref, feature_ref, distance_ref, along_ref, moved_ref,
-                   out_ref, total_ref, *buffers):
-    panels = distance_ref.shape[1]
+def spectra_kernel(core_ref, own_ref, other_ref, geom_ref, feature_ref, out_ref, total_ref,
+                   *buffers):
+    panels = own_ref.shape[3] // 2
     mics = feature_ref.shape[0]
     core = core_ref[0]
     total_ref[...] = jnp.zeros_like(total_ref)
 
     def block_of_panels(index, kernel_ref, weight_ref):
         here = pl.multiple_of(core * panels + index * tile, tile)
-        columns = pl.ds(pl.multiple_of(index * tile, tile), tile)
-        distance_rows, along_rows, moved_rows = (
-            ref[:, columns] for ref in (distance_ref, along_ref, moved_ref)
-        )
+        distance_rows, along_rows, moved_rows = panel_features(geom_ref[:, pl.ds(here, tile)])
 
         def both(part, kind):
             own = own_ref[part, kind, :, pl.ds(here, tile)]
@@ -168,33 +158,31 @@
 smem = pl.BlockSpec(memory_space=pltpu.SMEM)
 
 
-def prepared(core, geometry, mic_pos, order):
+def prepared(mic_pos, order):
     mics = mic_pos.shape[1]
-    panels = geometry.shape[1] // 2
-    rows = jax.ShapeDtypeStruct((64, panels), bf16)
     return pl.pallas_call(
-        prepare_kernel,
-        out_shape=[jax.ShapeDtypeStruct((mics, 64), bf16), rows, rows, rows],
-        in_specs=[smem] + [vmem] * 3,
-        out_specs=[vmem] * 4,
+        mic_features,
+        out_shape=jax.ShapeDtypeStruct((mics, 64), bf16),
+        in_specs=[vmem] * 2,
+        out_specs=vmem,
         compiler_params=pltpu.CompilerParams(vmem_limit_bytes=16 << 20),
         cost_estimate=pl.CostEstimate(
-            flops=2 * 10**9, bytes_accessed=3000000, transcendentals=0
+            flops=2 * 10**9, bytes_accessed=300000, transcendentals=0
         ),
-    )(core, geometry, mic_pos, order)
-
-
-def partial_spectra(core, own, other, features):
-    mics = features[0].shape[0]
+    )(order, mic_pos)
+
+
+def partial_spectra(core, own, other, geometry, features):
+    mics = features.shape[0]
     return pl.pallas_call(
         spectra_kernel,
         out_shape=jax.ShapeDtypeStruct((32, mics // 64, 128), f32),
-        in_specs=[smem] + [vmem] * 6,
+        in_specs=[smem] + [vmem] * 4,
         out_specs=vmem,
         scratch_shapes=[pltpu.VMEM((mics, 64), f32)]
         + [pltpu.VMEM((mics, 4 * tile), bf16), pltpu.VMEM((64, 4 * tile), bf16)] * 2,
         compiler_params=pltpu.CompilerParams(vmem_limit_bytes=32 << 20),
-    )(core, own, other, *features)
+    )(core, own, other, geometry, features)
 
 
 def shards(sources, panel_geom, mic_pos, mic_order):
@@ -202,8 +190,8 @@
     other = lax.ppermute(sources, "core", [(0, 1), (1, 0)])
     order = mic_order.reshape(2, 2, 32, 8).transpose(0, 2, 1, 3).reshape(1, -1)
     which = core.astype(jnp.int32).reshape(1)
-    features = prepared(which, panel_geom, mic_pos, order)
-    partial = partial_spectra(which, sources, other, features)
+    features = prepared(mic_pos, order)
+    partial = partial_spectra(which, sources, other, panel_geom, features)
     kept = jnp.sum(lax.all_to_all(partial, ("z", "x"), 0, 0, tiled=True), axis=0)
     quarters = kept.reshape(2, 8, 2, 64).transpose(2, 0, 1, 3).reshape(4, 8, 64)
     for_columns = jnp.repeat(quarters, 4, axis=0)

time: 90.8 us -> 88.3 us (0.972)
  Pallas kernels: 28.5 us -> 25.8 us
  waiting for transfers between devices: 9.55 us -> 10.6 us
    pallas_call x1, Pallas kernels: 27.4 us -> 25.3 us  [partial_spectra(): pl.pallas_call(spectra_kernel, out_shape=jax.ShapeDtypeStruct((32, mics /...]
    ppermute x1, waiting for transfers between devices: 0.01 us -> 1.03 us  [shards(): other = lax.ppermute(sources, 'core', [(0, 1), (1, 0)])]
  transfers between devices with their start and end apart: 2 -> 2, of which waited for: 1 -> 2; matrix products, arithmetic and copies ran while one was open for 1% -> 1% of each run, Pallas kernels for 1% -> 1%
where the time goes in v5:
time: 88.3 us; the launch traced here: 88 us
  blocking collectives  35.7 us (40%)
  Pallas kernels  25.8 us (29%)
  starting transfers between devices  12.8 us (14%)
  waiting for transfers between devices  10.6 us (12%)
  local copies, waits for them, and re-layouts  1.86 us (2%)
    pallas_call x1, Pallas kernels, partial_spectra(): pl.pallas_call(spectra_kernel, out_shape=jax.ShapeDtypeStruct((32, mics /...  25.3 us
    all_to_all x1, blocking collectives, shards(): lax.all_to_all(partial, ('z', 'x'), 0, 0, tiled=True)  18.9 us
    all_to_all x1, blocking collectives, shards(): terms = lax.all_to_all(terms, ('yh', 'core', 'yl'), 0, 0, tiled=True)  16.8 us
    all_to_all x1, waiting for transfers between devices, shards(): lax.all_to_all(spread, ('z', 'x'), 0, 0, tiled=True).reshape(256, 128)  9.55 us
    ppermute x1, starting transfers between devices, shards(): other = lax.ppermute(sources, 'core', [(0, 1), (1, 0)])  8.91 us
    all_to_all x1, starting transfers between devices, shards(): lax.all_to_all(spread, ('z', 'x'), 0, 0, tiled=True).reshape(256, 128)  3.84 us
  transfers between devices with their start and end apart: 2, of which 2 were waited for; matrix products, arithmetic and copies ran while one was open for 1% of the time, Pallas kernels for 1%

profile of v5, /device:TPU:1, one launch (start us, length us, event | category | flops | bytes accessed | tf_op | source)
XLA Modules:
  0.0 88.0 jit_solution(3175286771002825674)
XLA Ops:
  0.0 8.9 %collective-permute-start = (bf16[2,2,16,8192]{3,2,1,0:T(8,128)(2,1)}, bf16[2,2,16,8192]{3,2,1,0:T(8,128)(2,1)S(1)}, u32[]{:S(2)}, u32[]{:S(2)}) collective-permute-start(bf16[2,2,16,8192]{3,2,1,0:T(8,128)(2,1)} %own_ref.1), channel_id=1, source_target_pairs={{0,128},{128,0},{1,129},{129,1},{2,130},{130,2},{3,131},{131,3},{4... | collective-permute-start | bytes 3145736 | tf_op jit(solution)/shard_map/ppermute | solution.py:190
  8.9 0.0 copy-done.3
  8.9 0.1 reshape.34
  9.0 0.1 copy.11
  9.1 0.0 copy-start.2
  9.1 0.1 reshape.35.order_ref
  9.2 0.6 copy-done.2
  9.8 0.6 shard_map.46.feature_ref
  10.4 1.0 %collective-permute-done.other_ref = bf16[2,2,16,8192]{3,2,1,0:T(8,128)(2,1)S(1)} collective-permute-done((bf16[2,2,16,8192]{3,2,1,0:T(8,128)(2,1)}, bf16[2,2,16,8192]{3,2,1,0:T(8,128)(2,1)S(1)}, u32[]{:S(2)}, u32[]{:S(2)}) %collective-permute-start) | collective-permute-done | bytes 1048608 | tf_op jit(solution)/shard_map/ppermute | solution.py:190
  11.4 0.0 copy-done
  11.4 25.3 %shard_map.47 = f32[32,16,128]{2,1,0:T(8,128)S(1)} custom-call(s32[1]{0:T(128)} %bitcast.core_ref, bf16[2,2,16,8192]{3,2,1,0:T(8,128)(2,1)S(1)} %copy-done, bf16[2,2,16,8192]{3,2,1,0:T(8,128)(2,1)S(1)} %collective-permute-done.other_ref, f32[6,8192]{1,0:T(8,128)S(1)} %copy-done.1, bf16[1024,64]{1,0:T(8,128)(2,1)S(1)} %shard_map.46.feature_ref), custom_call_target="tpu_custom_call" | custom-call | tf_op jit(solution)/shard_map/pallas_call | solution.py:177
  36.7 18.9 %all_to_all.15 = f32[32,16,128]{2,1,0:T(8,128)S(1)} all-to-all(f32[32,16,128]{2,1,0:T(8,128)S(1)} %shard_map.47), channel_id=1, replica_groups=mesh['yh'=2,'core'=2,'yl'=4,'z'=8,'x'=4] {'z','x'}, dimensions={0} | all-to-all | bytes 524288 | tf_op jit(solution)/shard_map/all_to_all | solution.py:195
  55.6 0.1 reshape.36
  55.7 0.1 pad_maximum_fusion
  55.8 16.8 %all_to_all.16 = f32[16,8,128]{2,1,0:T(8,128)S(1)} all-to-all(f32[16,8,128]{2,1,0:T(8,128)S(1)} %pad_maximum_fusion), channel_id=1, replica_groups=mesh['yh'=2,'core'=2,'yl'=4,'z'=8,'x'=4] {'yh','core','yl'}, dimensions={0} | all-to-all | bytes 131072 | tf_op jit(solution)/shard_map/all_to_all | solution.py:200
  72.6 0.1 slice_bitcast_fusion
  72.7 0.1 broadcast_in_dim.11
  72.8 0.7 broadcast_in_dim.12
  73.5 3.8 %all-to-all-start.2 = ((f32[32,8,128]{2,1,0:T(8,128)}), f32[32,8,128]{2,1,0:T(8,128)S(1)}, u32[]{:S(2)}, u32[]{:S(2)}) async-start(f32[32,8,128]{2,1,0:T(8,128)} %broadcast_in_dim.12), calls=%async_computation.2 | async-start | bytes 262144 | tf_op jit(solution)/shard_map/all_to_all | solution.py:205
  77.3 0.1 fusion.1
  77.4 0.1 maximum_bitcast_fusion
  77.5 0.1 dot_general.5
  77.6 9.6 %all-to-all-done.2 = f32[32,8,128]{2,1,0:T(8,128)S(1)} async-done(((f32[32,8,128]{2,1,0:T(8,128)}), f32[32,8,128]{2,1,0:T(8,128)S(1)}, u32[]{:S(2)}, u32[]{:S(2)}) %all-to-all-start.2) | async-done | bytes 131104 | tf_op jit(solution)/shard_map/all_to_all | solution.py:205
  87.1 0.8 convolution_multiply_fusion
  (11 shorter events, 0.1 us)
Async XLA Ops:
  0.0 8.9 %copy-start.3 = (s32[1024]{0:T(1024)S(1)}, s32[1024]{0:T(1024)}, u32[]{:S(2)}) copy-start(s32[1024]{0:T(1024)} %param.7) | copy-start | bytes 12292
  0.0 11.4 %collective-permute-start = (bf16[2,2,16,8192]{3,2,1,0:T(8,128)(2,1)}, bf16[2,2,16,8192]{3,2,1,0:T(8,128)(2,1)S(1)}, u32[]{:S(2)}, u32[]{:S(2)}) collective-permute-start(bf16[2,2,16,8192]{3,2,1,0:T(8,128)(2,1)} %own_ref.1), channel_id=1, source_target_pairs={{0,128},{128,0},{1,129},{129,1},{2,130},{130,2},{3,131},{131,3},{4... | collective-permute-start | bytes 3145736 | tf_op jit(solution)/shard_map/ppermute | solution.py:190
  9.1 0.7 copy-start.2
  9.8 1.6 %copy-start = (bf16[2,2,16,8192]{3,2,1,0:T(8,128)(2,1)S(1)}, bf16[2,2,16,8192]{3,2,1,0:T(8,128)(2,1)}, u32[]{:S(2)}) copy-start(bf16[2,2,16,8192]{3,2,1,0:T(8,128)(2,1)} %own_ref.1) | copy-start | bytes 3145732
  9.8 1.6 %copy-start.1 = (f32[6,8192]{1,0:T(8,128)S(1)}, f32[6,8192]{1,0:T(8,128)}, u32[]{:S(2)}) copy-start(f32[6,8192]{1,0:T(8,128)} %geom_ref.1) | copy-start | bytes 589828
  73.5 13.7 %all-to-all-start.2 = ((f32[32,8,128]{2,1,0:T(8,128)}), f32[32,8,128]{2,1,0:T(8,128)S(1)}, u32[]{:S(2)}, u32[]{:S(2)}) async-start(f32[32,8,128]{2,1,0:T(8,128)} %broadcast_in_dim.12), calls=%async_computation.2 | async-start | bytes 262144 | tf_op jit(solution)/shard_map/all_to_all | solution.py:205

commit v6 on v5

--- a/solution.py
+++ b/solution.py
@@ -21,7 +21,7 @@
 PAN = ("yl", "z", "x")
 tile = 256
 chunk = 512
-unroll = 4
+unroll = 5
 
 
 def split3(value):
@@ -105,17 +105,31 @@
     return green_re, green_im, dip_re, dip_im
 
 
-def spectra_kernel(core_ref, own_ref, other_ref, geom_ref, feature_ref, out_ref, total_ref,
-                   *buffers):
+def fill_kernel(feature_ref, geometry, kernel_ref):
+    distance_rows, along_rows, moved_rows = panel_features(geometry)
+    for start in range(0, feature_ref.shape[0], chunk):
+        rows = slice(start, start + chunk)
+        features = feature_ref[rows]
+        distance = jnp.dot(features, distance_rows, preferred_element_type=f32)
+        moved = jnp.dot(features, moved_rows, preferred_element_type=f32)
+        along = jnp.dot(features, along_rows, preferred_element_type=f32)
+        for place, value in enumerate(kernel_values(distance, along, moved)):
+            kernel_ref[rows, place * tile : (place + 1) * tile] = value.astype(bf16)
+
+
+def first_kernel(core_ref, order_ref, mic_ref, geom_ref, feature_ref, kernel_ref):
+    mic_features(order_ref, mic_ref, feature_ref)
+    here = pl.multiple_of(core_ref[0] * (geom_ref.shape[1] // 2), tile)
+    fill_kernel(feature_ref, geom_ref[:, pl.ds(here, tile)], kernel_ref)
+
+
+def spectra_kernel(core_ref, own_ref, other_ref, geom_ref, feature_ref, first_ref, out_ref,
+                   total_ref, *buffers):
     panels = own_ref.shape[3] // 2
     mics = feature_ref.shape[0]
     core = core_ref[0]
-    total_ref[...] = jnp.zeros_like(total_ref)
-
-    def block_of_panels(index, kernel_ref, weight_ref):
-        here = pl.multiple_of(core * panels + index * tile, tile)
-        distance_rows, along_rows, moved_rows = panel_features(geom_ref[:, pl.ds(here, tile)])
-
+
+    def fill_weights(here, weight_ref):
         def both(part, kind):
             own = own_ref[part, kind, :, pl.ds(here, tile)]
             other = other_ref[part, kind, :, pl.ds(here, tile)]
@@ -130,25 +144,26 @@
         )
         for place, block in enumerate(blocks):
             weight_ref[:, place * tile : (place + 1) * tile] = jnp.concatenate(block, 0)
-        for start in range(0, mics, chunk):
-            rows = slice(start, start + chunk)
-            features = feature_ref[rows]
-            distance = jnp.dot(features, distance_rows, preferred_element_type=f32)
-            moved = jnp.dot(features, moved_rows, preferred_element_type=f32)
-            along = jnp.dot(features, along_rows, preferred_element_type=f32)
-            for place, value in enumerate(kernel_values(distance, along, moved)):
-                kernel_ref[rows, place * tile : (place + 1) * tile] = value.astype(bf16)
-        total_ref[...] += lax.dot_general(
+
+    def product(kernel_ref, weight_ref):
+        return lax.dot_general(
             kernel_ref[...], weight_ref[...], (((1,), (1,)), ((), ())), preferred_element_type=f32
         )
+
+    fill_weights(pl.multiple_of(core * panels, tile), buffers[1])
+    total_ref[...] = product(first_ref, buffers[1])
 
     def step(index, carry):
         for part in range(unroll):
             kernel_ref, weight_ref = buffers[2 * (part % 2) : 2 * (part % 2) + 2]
-            block_of_panels(unroll * index + part, kernel_ref, weight_ref)
+            block = unroll * index + part + 1
+            here = pl.multiple_of(core * panels + block * tile, tile)
+            fill_weights(here, weight_ref)
+            fill_kernel(feature_ref, geom_ref[:, pl.ds(here, tile)], kernel_ref)
+            total_ref[...] += product(kernel_ref, weight_ref)
         return carry
 
-    lax.fori_loop(0, panels // (unroll * tile), step, 0)
+    lax.fori_loop(0, (panels // tile - 1) // unroll, step, 0)
     half = mics // 2
     both_halves = jnp.concatenate([total_ref[:half], total_ref[half:]], 1)
     out_ref[...] = both_halves.reshape(out_ref.shape)
@@ -158,31 +173,34 @@
 smem = pl.BlockSpec(memory_space=pltpu.SMEM)
 
 
-def prepared(mic_pos, order):
+def prepared(core, geometry, mic_pos, order):
     mics = mic_pos.shape[1]
     return pl.pallas_call(
-        mic_features,
-        out_shape=jax.ShapeDtypeStruct((mics, 64), bf16),
-        in_specs=[vmem] * 2,
-        out_specs=vmem,
+        first_kernel,
+        out_shape=[
+            jax.ShapeDtypeStruct((mics, 64), bf16),
+            jax.ShapeDtypeStruct((mics, 4 * tile), bf16),
+        ],
+        in_specs=[smem] + [vmem] * 3,
+        out_specs=[vmem] * 2,
         compiler_params=pltpu.CompilerParams(vmem_limit_bytes=16 << 20),
         cost_estimate=pl.CostEstimate(
-            flops=2 * 10**9, bytes_accessed=300000, transcendentals=0
+            flops=2 * 10**9, bytes_accessed=3000000, transcendentals=0
         ),
-    )(order, mic_pos)
-
-
-def partial_spectra(core, own, other, geometry, features):
+    )(core, order, mic_pos, geometry)
+
+
+def partial_spectra(core, own, other, geometry, features, first):
     mics = features.shape[0]
     return pl.pallas_call(
         spectra_kernel,
         out_shape=jax.ShapeDtypeStruct((32, mics // 64, 128), f32),
-        in_specs=[smem] + [vmem] * 4,
+        in_specs=[smem] + [vmem] * 5,
         out_specs=vmem,
         scratch_shapes=[pltpu.VMEM((mics, 64), f32)]
         + [pltpu.VMEM((mics, 4 * tile), bf16), pltpu.VMEM((64, 4 * tile), bf16)] * 2,
         compiler_params=pltpu.CompilerParams(vmem_limit_bytes=32 << 20),
-    )(core, own, other, geometry, features)
+    )(core, own, other, geometry, features, first)
 
 
 def shards(sources, panel_geom, mic_pos, mic_order):
@@ -190,8 +208,8 @@
     other = lax.ppermute(sources, "core", [(0, 1), (1, 0)])
     order = mic_order.reshape(2, 2, 32, 8).transpose(0, 2, 1, 3).reshape(1, -1)
     which = core.astype(jnp.int32).reshape(1)
-    features = prepared(mic_pos, order)
-    partial = partial_spectra(which, sources, other, panel_geom, features)
+    features, first = prepared(which, panel_geom, mic_pos, order)
+    partial = partial_spectra(which, sources, other, panel_geom, features, first)
     kept = jnp.sum(lax.all_to_all(partial, ("z", "x"), 0, 0, tiled=True), axis=0)
     quarters = kept.reshape(2, 8, 2, 64).transpose(2, 0, 1, 3).reshape(4, 8, 64)
     for_columns = jnp.repeat(quarters, 4, axis=0)
@@ -203,6 +221,7 @@
     own_columns = joined[:, :, :64].transpose(1, 0, 2).reshape(8, 128)
     spread = jnp.broadcast_to(own_columns[None], (32, 8, 128))
     columns = lax.all_to_all(spread, ("z", "x"), 0, 0, tiled=True).reshape(256, 128)
+    rows, columns = lax.optimization_barrier((rows, columns))
     turned = jnp.concatenate([rows[..., 32:], -rows[..., :32]], 2)
     left = jnp.concatenate([rows, turned], 1).transpose(1, 0, 2).reshape(16, 128)
     csm = lax.dot_general(

time: 88.3 us -> 87.9 us (level)
  blocking collectives: 35.7 us -> 48.4 us
  waiting for transfers between devices: 10.6 us -> 0.01 us
  starting transfers between devices: 12.8 us -> 8.78 us
  local copies, waits for them, and re-layouts: 1.86 us -> 3 us
    all_to_all x0 -> x1, blocking collectives: none -> 12.6 us  [shards(): lax.all_to_all(spread, ('z', 'x'), 0, 0, tiled=True).reshape(256, 128)]
    all_to_all x1 -> x0, waiting for transfers between devices: 9.55 us -> none  [shards(): lax.all_to_all(spread, ('z', 'x'), 0, 0, tiled=True).reshape(256, 128)]
    all_to_all x1 -> x0, starting transfers between devices: 3.84 us -> none  [shards(): lax.all_to_all(spread, ('z', 'x'), 0, 0, tiled=True).reshape(256, 128)]
    pallas_call x1, Pallas kernels: 0.55 us -> 1.67 us  [prepared(): pl.pallas_call(first_kernel, out_shape=[jax.ShapeDtypeStruct((mics, 64),...]
    unnamed x8, local copies, waits for them, and re-layouts: 0.59 us -> 1.68 us
    ppermute x1, waiting for transfers between devices: 1.03 us -> 0.01 us  [shards(): other = lax.ppermute(sources, 'core', [(0, 1), (1, 0)])]
  transfers between devices with their start and end apart: 2 -> 1, of which waited for: 2 -> 0; matrix products, arithmetic and copies ran while one was open for 1% -> 1% of each run, Pallas kernels for 1% -> 2%
where the time goes in v6:
time: 87.9 us; the launch traced here: 87.5 us
  blocking collectives  48.4 us (55%)
  Pallas kernels  26.1 us (30%)
  starting transfers between devices  8.78 us (10%)
  local copies, waits for them, and re-layouts  3 us (3%)
    pallas_call x1, Pallas kernels, partial_spectra(): pl.pallas_call(spectra_kernel, out_shape=jax.ShapeDtypeStruct((32, mics /...  24.5 us
    all_to_all x1, blocking collectives, shards(): lax.all_to_all(partial, ('z', 'x'), 0, 0, tiled=True)  19.3 us
    all_to_all x1, blocking collectives, shards(): terms = lax.all_to_all(terms, ('yh', 'core', 'yl'), 0, 0, tiled=True)  16.5 us
    all_to_all x1, blocking collectives, shards(): lax.all_to_all(spread, ('z', 'x'), 0, 0, tiled=True).reshape(256, 128)  12.6 us
    ppermute x1, starting transfers between devices, shards(): other = lax.ppermute(sources, 'core', [(0, 1), (1, 0)])  8.78 us
  transfers between devices with their start and end apart: 1, of which 0 were waited for; matrix products, arithmetic and copies ran while one was open for 1% of the time, Pallas kernels for 2%

profile of v6, /device:TPU:1, one launch (start us, length us, event | category | flops | bytes accessed | tf_op | source)
XLA Modules:
  0.0 87.5 jit_solution(13918912873953158572)
XLA Ops:
  0.0 8.8 %collective-permute-start = (bf16[2,2,16,8192]{3,2,1,0:T(8,128)(2,1)}, bf16[2,2,16,8192]{3,2,1,0:T(8,128)(2,1)S(1)}, u32[]{:S(2)}, u32[]{:S(2)}) collective-permute-start(bf16[2,2,16,8192]{3,2,1,0:T(8,128)(2,1)} %own_ref.1), channel_id=1, source_target_pairs={{0,128},{128,0},{1,129},{129,1},{2,130},{130,2},{3,131},{131,3},{4... | collective-permute-start | bytes 3145736 | tf_op jit(solution)/shard_map/ppermute | solution.py:208
  8.8 0.8 reshape.34
  9.6 0.1 copy.11
  9.6 0.1 reshape.35.order_ref
  9.8 0.0 copy-start.1
  9.8 1.0 %copy-done.1 = f32[6,8192]{1,0:T(8,128)S(1)} copy-done((f32[6,8192]{1,0:T(8,128)S(1)}, f32[6,8192]{1,0:T(8,128)}, u32[]{:S(2)}) %copy-start.1) | copy-done | bytes 196632
  10.7 0.0 copy-start.3
  10.7 0.7 copy-done.3
  11.4 1.7 %shard_map.46 = (bf16[1024,64]{1,0:T(8,128)(2,1)S(1)}, bf16[1024,1024]{1,0:T(8,128)(2,1)S(1)}) custom-call(s32[1]{0:T(128)} %bitcast.core_ref, s32[1,1024]{1,0:T(1,128)S(1)} %reshape.35.order_ref, f32[3,1024]{1,0:T(4,128)S(1)} %copy-done.3, f32[6,8192]{1,0:T(8,128)S(1)} %copy-done.1), custom_call_target="tpu_custom_call" | custom-call | flops 2000000000 | bytes 3000000 | tf_op jit(solution)/shard_map/pallas_call | solution.py:178
  13.1 0.0 collective-permute-done.other_ref
  13.1 0.0 copy-done
  13.1 0.0 copy-done.2
  13.2 24.5 %shard_map.47 = f32[32,16,128]{2,1,0:T(8,128)S(1)} custom-call(s32[1]{0:T(128)} %bitcast.core_ref, bf16[2,2,16,8192]{3,2,1,0:T(8,128)(2,1)S(1)} %copy-done, bf16[2,2,16,8192]{3,2,1,0:T(8,128)(2,1)S(1)} %collective-permute-done.other_ref, f32[6,8192]{1,0:T(8,128)S(1)} %copy-done.2, bf16[1024,64]{1,0:T(8,128)(2,1)S(1)} %get-tuple-element.9.feature_ref, ...), custom_call_target="tpu_custom_call" | custom-call | tf_op jit(solution)/shard_map/pallas_call | solution.py:195
  37.6 19.3 %all_to_all.15 = f32[32,16,128]{2,1,0:T(8,128)S(1)} all-to-all(f32[32,16,128]{2,1,0:T(8,128)S(1)} %shard_map.47), channel_id=1, replica_groups=mesh['yh'=2,'core'=2,'yl'=4,'z'=8,'x'=4] {'z','x'}, dimensions={0} | all-to-all | bytes 524288 | tf_op jit(solution)/shard_map/all_to_all | solution.py:213
  57.0 0.1 reshape.36
  57.1 0.1 pad_maximum_fusion
  57.2 16.5 %all_to_all.16 = f32[16,8,128]{2,1,0:T(8,128)S(1)} all-to-all(f32[16,8,128]{2,1,0:T(8,128)S(1)} %pad_maximum_fusion), channel_id=1, replica_groups=mesh['yh'=2,'core'=2,'yl'=4,'z'=8,'x'=4] {'yh','core','yl'}, dimensions={0} | all-to-all | bytes 131072 | tf_op jit(solution)/shard_map/all_to_all | solution.py:218
  73.7 0.1 slice_bitcast_fusion
  73.8 0.1 broadcast_in_dim.11
  73.9 12.6 %all_to_all.17 = f32[32,8,128]{2,1,0:T(8,128)S(1)} all-to-all(f32[32,8,128]{2,1,0:T(8,128)S(1)} %broadcast_in_dim.12), channel_id=1, replica_groups=mesh['yh'=2,'core'=2,'yl'=4,'z'=8,'x'=4] {'z','x'}, dimensions={0} | all-to-all | bytes 262144 | tf_op jit(solution)/shard_map/all_to_all | solution.py:223
  86.5 0.1 fusion.1
  86.5 0.1 maximum_bitcast_fusion
  86.6 0.1 dot_general.5
  86.7 0.8 convolution_multiply_fusion
  (10 shorter events, 0.1 us)
Async XLA Ops:
  0.0 13.1 %collective-permute-start = (bf16[2,2,16,8192]{3,2,1,0:T(8,128)(2,1)}, bf16[2,2,16,8192]{3,2,1,0:T(8,128)(2,1)S(1)}, u32[]{:S(2)}, u32[]{:S(2)}) collective-permute-start(bf16[2,2,16,8192]{3,2,1,0:T(8,128)(2,1)} %own_ref.1), channel_id=1, source_target_pairs={{0,128},{128,0},{1,129},{129,1},{2,130},{130,2},{3,131},{131,3},{4... | collective-permute-start | bytes 3145736 | tf_op jit(solution)/shard_map/ppermute | solution.py:208
  9.8 1.0 %copy-start.1 = (f32[6,8192]{1,0:T(8,128)S(1)}, f32[6,8192]{1,0:T(8,128)}, u32[]{:S(2)}) copy-start(f32[6,8192]{1,0:T(8,128)} %geom_ref.3) | copy-start | bytes 589828
  10.7 0.7 copy-start.3
  11.4 1.7 %copy-start = (bf16[2,2,16,8192]{3,2,1,0:T(8,128)(2,1)S(1)}, bf16[2,2,16,8192]{3,2,1,0:T(8,128)(2,1)}, u32[]{:S(2)}) copy-start(bf16[2,2,16,8192]{3,2,1,0:T(8,128)(2,1)} %own_ref.1) | copy-start | bytes 3145732
  11.4 1.7 %copy-start.2 = (f32[6,8192]{1,0:T(8,128)S(1)}, f32[6,8192]{1,0:T(8,128)}, u32[]{:S(2)}) copy-start(f32[6,8192]{1,0:T(8,128)} %geom_ref.3) | copy-start | bytes 589828

commit v7 on v5

--- a/solution.py
+++ b/solution.py
@@ -35,7 +35,7 @@
     return jnp.zeros((count, width), f32)
 
 
-def mic_features(order_ref, mic_ref, feature_ref):
+def mic_features(order_ref, mic_ref, feature_ref, placed_ref):
     mics = mic_ref[...]
     total = mics.shape[1]
     parts = jnp.concatenate([*split3(mics), zero_rows(7, total)], 0).astype(bf16)
@@ -53,7 +53,9 @@
         ones = jnp.ones((3, tile), f32)
         rows = [high, high, middle, high, middle, low, ones, *split3(square), *split3(shift)]
         rows.append(zero_rows(37, tile))
-        feature_ref[start : start + tile, :] = jnp.concatenate(rows, 0).T.astype(bf16)
+        yl = start // tile
+        placed_ref[yl // 2, :, yl % 2] = jnp.concatenate(rows, 0).T.reshape(-1, 8, 64)
+    feature_ref[...] = placed_ref[...].reshape(total, 64).astype(bf16)
 
 
 def panel_features(geometry):
@@ -165,6 +167,7 @@
         out_shape=jax.ShapeDtypeStruct((mics, 64), bf16),
         in_specs=[vmem] * 2,
         out_specs=vmem,
+        scratch_shapes=[pltpu.VMEM((2, mics // 32, 2, 8, 64), f32)],
         compiler_params=pltpu.CompilerParams(vmem_limit_bytes=16 << 20),
         cost_estimate=pl.CostEstimate(
             flops=2 * 10**9, bytes_accessed=300000, transcendentals=0
@@ -188,7 +191,7 @@
 def shards(sources, panel_geom, mic_pos, mic_order):
     core = lax.axis_index("core")
     other = lax.ppermute(sources, "core", [(0, 1), (1, 0)])
-    order = mic_order.reshape(2, 2, 32, 8).transpose(0, 2, 1, 3).reshape(1, -1)
+    order = mic_order.reshape(1, -1)
     which = core.astype(jnp.int32).reshape(1)
     features = prepared(mic_pos, order)
     partial = partial_spectra(which, sources, other, panel_geom, features)
@@ -203,6 +206,7 @@
     own_columns = joined[:, :, :64].transpose(1, 0, 2).reshape(8, 128)
     spread = jnp.broadcast_to(own_columns[None], (32, 8, 128))
     columns = lax.all_to_all(spread, ("z", "x"), 0, 0, tiled=True).reshape(256, 128)
+    rows, columns = lax.optimization_barrier((rows, columns))
     turned = jnp.concatenate([rows[..., 32:], -rows[..., :32]], 2)
     left = jnp.concatenate([rows, turned], 1).transpose(1, 0, 2).reshape(16, 128)
     csm = lax.dot_general(

time: 88.3 us -> 87 us (0.985)
  blocking collectives: 35.7 us -> 48.4 us
  waiting for transfers between devices: 10.6 us -> 0.45 us
  starting transfers between devices: 12.8 us -> 8.77 us
    all_to_all x0 -> x1, blocking collectives: none -> 12.6 us  [shards(): lax.all_to_all(spread, ('z', 'x'), 0, 0, tiled=True).reshape(256, 128)]
    all_to_all x1 -> x0, waiting for transfers between devices: 9.55 us -> none  [shards(): lax.all_to_all(spread, ('z', 'x'), 0, 0, tiled=True).reshape(256, 128)]
    all_to_all x1 -> x0, starting transfers between devices: 3.84 us -> none  [shards(): lax.all_to_all(spread, ('z', 'x'), 0, 0, tiled=True).reshape(256, 128)]
    unnamed x8, local copies, waits for them, and re-layouts: 0.59 us -> 1.59 us
  transfers between devices with their start and end apart: 2 -> 1, of which waited for: 2 -> 1; matrix products, arithmetic and copies ran while one was open for 1% -> 0% of each run, Pallas kernels for 1% -> 1%
where the time goes in v7:
time: 87 us; the launch traced here: 86.7 us
  blocking collectives  48.4 us (56%)
  Pallas kernels  25.9 us (30%)
  starting transfers between devices  8.77 us (10%)
  local copies, waits for them, and re-layouts  1.96 us (2%)
    pallas_call x1, Pallas kernels, partial_spectra(): pl.pallas_call(spectra_kernel, out_shape=jax.ShapeDtypeStruct((32, mics /...  25.3 us
    all_to_all x1, blocking collectives, shards(): lax.all_to_all(partial, ('z', 'x'), 0, 0, tiled=True)  19.1 us
    all_to_all x1, blocking collectives, shards(): terms = lax.all_to_all(terms, ('yh', 'core', 'yl'), 0, 0, tiled=True)  16.7 us
    all_to_all x1, blocking collectives, shards(): lax.all_to_all(spread, ('z', 'x'), 0, 0, tiled=True).reshape(256, 128)  12.6 us
    ppermute x1, starting transfers between devices, shards(): other = lax.ppermute(sources, 'core', [(0, 1), (1, 0)])  8.77 us
  transfers between devices with their start and end apart: 1, of which 1 were waited for; matrix products, arithmetic and copies ran while one was open for 0% of the time, Pallas kernels for 1%

profile of v7, /device:TPU:1, one launch (start us, length us, event | category | flops | bytes accessed | tf_op | source)
XLA Modules:
  0.0 86.7 jit_solution(12894012349715372381)
XLA Ops:
  0.0 8.8 %collective-permute-start = (bf16[2,2,16,8192]{3,2,1,0:T(8,128)(2,1)}, bf16[2,2,16,8192]{3,2,1,0:T(8,128)(2,1)S(1)}, u32[]{:S(2)}, u32[]{:S(2)}) collective-permute-start(bf16[2,2,16,8192]{3,2,1,0:T(8,128)(2,1)} %own_ref.1), channel_id=1, source_target_pairs={{0,128},{128,0},{1,129},{129,1},{2,130},{130,2},{3,131},{131,3},{4... | collective-permute-start | bytes 3145736 | tf_op jit(solution)/shard_map/ppermute | solution.py:193
  8.8 0.0 copy-start.3
  8.8 0.7 copy-done.3
  9.5 0.0 copy-start.2
  9.5 0.7 copy-done.2
  10.2 0.0 copy-start
  10.2 0.0 copy-start.1
  10.2 0.6 shard_map.46.feature_ref
  10.8 0.4 collective-permute-done.other_ref
  11.3 0.2 copy-done
  11.4 0.0 copy-done.1
  11.5 25.3 %shard_map.47 = f32[32,16,128]{2,1,0:T(8,128)S(1)} custom-call(s32[1]{0:T(128)} %bitcast.core_ref, bf16[2,2,16,8192]{3,2,1,0:T(8,128)(2,1)S(1)} %copy-done, bf16[2,2,16,8192]{3,2,1,0:T(8,128)(2,1)S(1)} %collective-permute-done.other_ref, f32[6,8192]{1,0:T(8,128)S(1)} %copy-done.1, bf16[1024,64]{1,0:T(8,128)(2,1)S(1)} %shard_map.46.feature_ref), custom_call_target="tpu_custom_call" | custom-call | tf_op jit(solution)/shard_map/pallas_call | solution.py:180
  36.8 19.1 %all_to_all.15 = f32[32,16,128]{2,1,0:T(8,128)S(1)} all-to-all(f32[32,16,128]{2,1,0:T(8,128)S(1)} %shard_map.47), channel_id=1, replica_groups=mesh['yh'=2,'core'=2,'yl'=4,'z'=8,'x'=4] {'z','x'}, dimensions={0} | all-to-all | bytes 524288 | tf_op jit(solution)/shard_map/all_to_all | solution.py:198
  55.9 0.1 reshape.32
  56.0 0.1 pad_maximum_fusion
  56.1 16.7 %all_to_all.16 = f32[16,8,128]{2,1,0:T(8,128)S(1)} all-to-all(f32[16,8,128]{2,1,0:T(8,128)S(1)} %pad_maximum_fusion), channel_id=1, replica_groups=mesh['yh'=2,'core'=2,'yl'=4,'z'=8,'x'=4] {'yh','core','yl'}, dimensions={0} | all-to-all | bytes 131072 | tf_op jit(solution)/shard_map/all_to_all | solution.py:203
  72.8 0.1 slice_bitcast_fusion
  72.9 0.1 broadcast_in_dim.11
  73.0 12.6 %all_to_all.17 = f32[32,8,128]{2,1,0:T(8,128)S(1)} all-to-all(f32[32,8,128]{2,1,0:T(8,128)S(1)} %broadcast_in_dim.12), channel_id=1, replica_groups=mesh['yh'=2,'core'=2,'yl'=4,'z'=8,'x'=4] {'z','x'}, dimensions={0} | all-to-all | bytes 262144 | tf_op jit(solution)/shard_map/all_to_all | solution.py:208
  85.6 0.1 fusion.1
  85.7 0.1 maximum_bitcast_fusion
  85.8 0.1 dot_general.5
  85.8 0.8 convolution_multiply_fusion
  (8 shorter events, 0.1 us)
Async XLA Ops:
  0.0 11.3 %collective-permute-start = (bf16[2,2,16,8192]{3,2,1,0:T(8,128)(2,1)}, bf16[2,2,16,8192]{3,2,1,0:T(8,128)(2,1)S(1)}, u32[]{:S(2)}, u32[]{:S(2)}) collective-permute-start(bf16[2,2,16,8192]{3,2,1,0:T(8,128)(2,1)} %own_ref.1), channel_id=1, source_target_pairs={{0,128},{128,0},{1,129},{129,1},{2,130},{130,2},{3,131},{131,3},{4... | collective-permute-start | bytes 3145736 | tf_op jit(solution)/shard_map/ppermute | solution.py:193
  8.8 0.7 copy-start.3
  9.5 0.7 copy-start.2
  10.2 1.2 %copy-start = (bf16[2,2,16,8192]{3,2,1,0:T(8,128)(2,1)S(1)}, bf16[2,2,16,8192]{3,2,1,0:T(8,128)(2,1)}, u32[]{:S(2)}) copy-start(bf16[2,2,16,8192]{3,2,1,0:T(8,128)(2,1)} %own_ref.1) | copy-start | bytes 3145732
  10.2 1.3 %copy-start.1 = (f32[6,8192]{1,0:T(8,128)S(1)}, f32[6,8192]{1,0:T(8,128)}, u32[]{:S(2)}) copy-start(f32[6,8192]{1,0:T(8,128)} %geom_ref.1) | copy-start | bytes 589828
